TPU v7x, 32 devices: a whole 2x2x4 slice. The times are simulated.
32 devices in a mesh: batch: 4 (over x, core), hidden: 2 (over y), width: 4 (over z).
Axes of the slice: x: 2, y: 2, z: 4, core: 2. Of those that a mesh axis runs over, the one named last changes fastest.
Arguments:
- frames: bfloat16 [4, 512, 1280], P('batch', None, 'hidden'), may hold values from -6 to 6
- adapter_weight: bfloat16 [4, 1280, 16384], P(None, 'hidden', 'width'), may hold values from -0.078125 to 0.078125
- text_embed: bfloat16 [512, 16384], P('batch', 'width'), may hold values from -6 to 6
- audio_len: int32 [4], P('batch'), may hold values from 16 to 64, as said below
- text_len: int32 [4], P('batch'), may hold values from 32 to 112, as said below
- norm_gain: bfloat16 [16384], P('width'), may hold values from 0.5 to 1.5
- gate_up: bfloat16 [16384, 2, 26624], P('width', None, ('batch', 'hidden')), may hold values from -0.046875 to 0.046875
- cotangent: bfloat16 [512, 26624], P('width', ('batch', 'hidden')), may hold values from -0.59765625 to 0.59765625
Outputs:
- hidden: bfloat16 [512, 26624], P('width', ('batch', 'hidden'))
- weight_grad: float32 [4, 1280, 16384], P(None, 'hidden', 'width')
Inputs may be any that keep to these rules, and one draw needn't show every extreme that they name: `audio_len`: some sequence holds exactly 16 audio positions and another exactly 64. audio_len + text_len never exceeds 128, and equals it in some sequence.
All inputs are finite; a program needn't handle non-finite values.
Results may differ from a plain program's by a relative error of at most 0.0059.
Values may be sent and summed in bfloat16 or wider, within the bound.
No kernel may reach another device: no remote copies, remote signals or barrier semaphores. Data moves between devices by JAX's collectives and lax.ppermute only.
A program may use at most 256 MiB of HBM per device.

v0:
```python
import jax
import jax.numpy as jnp
from jax import lax
from jax.sharding import PartitionSpec as P

D = 16384


norm_eps = 1e-05


def row_lookup(table, row_index):
    slots = jnp.arange(table.shape[0], dtype=jnp.int32)
    return jnp.sum(jnp.where(row_index[:, None] == slots[None, :], table[None, :], 0), axis=1)


def on_device(
    frames, adapter_weight, text_embed, audio_len, text_len, norm_gain, gate_up, cotangent
):
    rows_here, frame_count, feat_here = frames.shape
    seq_len = frame_count // 4
    width_here = adapter_weight.shape[2]
    tok_here = rows_here * seq_len
    stacked = frames.reshape(tok_here, 4 * feat_here)
    kernel = adapter_weight.reshape(4 * feat_here, width_here)
    partial_audio = jnp.dot(stacked, kernel, preferred_element_type=jnp.float32)
    audio_part = lax.psum(partial_audio, "hidden")
    local_index = jnp.arange(tok_here, dtype=jnp.int32)
    row_index = local_index // seq_len
    positions = local_index % seq_len
    audio_count = row_lookup(audio_len, row_index)
    text_count = row_lookup(text_len, row_index)
    is_audio = positions < audio_count
    is_text = jnp.logical_and(jnp.logical_not(is_audio), positions < audio_count + text_count)
    stream = jnp.where(
        is_audio[:, None],
        audio_part,
        jnp.where(is_text[:, None], text_embed.astype(jnp.float32), jnp.zeros_like(audio_part)),
    )
    sum_squares = lax.psum(jnp.sum(stream * stream, axis=1), "width")
    inv_rms = lax.rsqrt(sum_squares / D + norm_eps)
    unit_stream = stream * inv_rms[:, None]
    gain_vals = norm_gain.astype(jnp.float32)
    normed = (unit_stream * gain_vals[None, :]).astype(jnp.bfloat16)
    weights = gate_up.reshape(width_here, -1)
    half_cols = weights.shape[1] // 2
    partial_pair = jnp.dot(
        lax.all_gather(normed, "batch", axis=0, tiled=True),
        weights,
        preferred_element_type=jnp.float32,
    )
    summed = lax.psum_scatter(partial_pair, "width", scatter_dimension=0, tiled=True)
    gate_vals = summed[:, :half_cols]
    up_vals = summed[:, half_cols:]
    sigmoid_gate = jax.nn.sigmoid(gate_vals)
    silu_gate = gate_vals * sigmoid_gate
    hidden = (silu_gate * up_vals).astype(jnp.bfloat16)
    cot_vals = cotangent.astype(jnp.float32)
    silu_slope = sigmoid_gate * (1.0 + gate_vals * (1.0 - sigmoid_gate))
    grad_pair = jnp.concatenate(
        [
            (cot_vals * up_vals * silu_slope).astype(jnp.bfloat16),
            (cot_vals * silu_gate).astype(jnp.bfloat16),
        ],
        axis=1,
    )
    all_pairs = lax.all_gather(grad_pair, "width", axis=0, tiled=True)
    share_rows = tok_here // lax.axis_size("hidden")
    row_block = all_pairs
    normed_grad = lax.psum_scatter(
        lax.dot_general(
            row_block, weights, (((1,), (1,)), ((), ())), preferred_element_type=jnp.float32
        ),
        ("batch", "hidden"),
        scatter_dimension=0,
        tiled=True,
    )
    share_start = lax.axis_index("hidden") * share_rows
    unit_share = lax.dynamic_slice_in_dim(unit_stream, share_start, share_rows, 0)
    inv_share = lax.dynamic_slice_in_dim(inv_rms, share_start, share_rows, 0)
    audio_share = lax.dynamic_slice_in_dim(is_audio, share_start, share_rows, 0)
    scaled_grad = normed_grad * gain_vals[None, :]
    proj_stat = lax.psum(jnp.sum(unit_share * scaled_grad, axis=1), "width") / D
    stream_grad = (scaled_grad - unit_share * proj_stat[:, None]) * inv_share[:, None]
    audio_grad = jnp.where(audio_share[:, None], stream_grad, jnp.zeros_like(stream_grad)).astype(
        jnp.bfloat16
    )
    all_frames = lax.all_gather(frames, "batch", axis=0, tiled=True)
    all_stacked = all_frames.reshape(-1, 4 * feat_here)
    row_block = all_stacked
    weight_grad = lax.dot_general(
        row_block,
        lax.all_gather(audio_grad, ("batch", "hidden"), axis=0, tiled=True),
        (((0,), (0,)), ((), ())),
        preferred_element_type=jnp.float32,
    )
    return (hidden, weight_grad.reshape(4, feat_here, width_here))


def solution(mesh):
    return jax.shard_map(
        on_device,
        mesh=mesh,
        in_specs=(
            P("batch", None, "hidden"),
            P(None, "hidden", "width"),
            P("batch", "width"),
            P("batch"),
            P("batch"),
            P("width"),
            P("width", None, ("batch", "hidden")),
            P("width", ("batch", "hidden")),
        ),
        out_specs=(P("width", ("batch", "hidden")), P(None, "hidden", "width")),
        check_vma=False,
    )
```

profile of v0, /device:TPU:0, one launch (start us, length us, event | category | flops | bytes accessed | tf_op | source)
XLA Modules:
  0.0 737.0 jit_solution(10051445883625385876)
XLA Ops:
  7.2 0.0 all-reduce.2.cloned.1.call-start
  7.2 1.5 reshape.67
  8.7 11.2 %fusion.8 = f32[128,4096]{1,0:T(8,128)} fusion(bf16[128,2560]{1,0:T(8,128)(2,1)S(1)} %reshape.67, bf16[2560,4096]{1,0:T(8,128)(2,1)} %bitcast.21), kind=kOutput, calls=%fused_computation.27 | convolution fusion | flops 2684354560 | bytes 23724032 | tf_op jit(solution)/shard_map/dot_general | solution.py:26
  19.9 0.0 all-reduce.2.cloned.1.call-update
  19.9 0.0 all-gather.5.cloned.1.call-start
  21.4 64.4 %all-reduce.2.cloned.1.call-done = f32[128,4096]{1,0:T(8,128)} async-done(((f32[128,4096]{1,0:T(8,128)}), f32[128,4096]{1,0:T(8,128)}) %all-reduce.2.cloned.1.call-update) | async-done | bytes 2097168 | tf_op jit(solution)/shard_map/psum | solution.py:27
  85.8 2.1 multiply_reduce_fusion
  87.9 11.7 %psum.22 = f32[128]{0:T(128)S(1)} all-reduce(f32[128]{0:T(128)S(1)} %multiply_reduce_fusion), channel_id=1, replica_groups=mesh['batch'=4,'hidden'=2,'width'=4] {'width'}, use_global_device_ids=true, to_apply=%region_2.3 | all-reduce | flops 128 | bytes 1024 | tf_op jit(solution)/shard_map/psum | solution.py:40
  99.6 3.2 multiply_convert_fusion
  102.8 0.0 reduce-scatter.3.cloned.1.call-start
  102.8 37.4 %copy.10 = bf16[512,8,2,3328]{3,1,2,0:T(8,128)(2,1)} copy(bf16[512,8,2,3328]{3,2,1,0:T(2,128)(2,1)} %bitcast.18) | data formatting | bytes 109051904
  140.2 38.9 %fusion.9 = f32[512,6656]{1,0:T(8,128)} fusion(bf16[512,4096]{1,0:T(8,128)(2,1)} %all-gather.5.cloned.1.call-done, bf16[4096,6656]{1,0:T(8,128)(2,1)} %bitcast.19), kind=kOutput, calls=%fused_computation.28 | convolution fusion | flops 27917287424 | bytes 72351744 | tf_op jit(solution)/shard_map/dot_general | solution.py:47
  179.1 0.2 all-gather.7.cloned.1.call-start
  179.4 226.3 %reduce-scatter.3.cloned.1.call-done = f32[128,6656]{1,0:T(8,128)} async-done(((f32[512,6656]{1,0:T(8,128)}), f32[128,6656]{1,0:T(8,128)}) %reduce-scatter.3.cloned.1.call-update) | async-done | bytes 3407888 | tf_op jit(solution)/shard_map/reduce_scatter | solution.py:52
  405.7 3.9 fusion.1
  409.5 1.3 pad_maximum_fusion
  410.9 0.0 reduce-scatter.5.cloned.1.call-start
  410.9 125.0 %all-gather.7.cloned.1.call-done = bf16[512,6656]{1,0:T(8,128)(2,1)} async-done(((bf16[128,6656]{1,0:T(8,128)(2,1)}), bf16[512,6656]{1,0:T(8,128)(2,1)}) %all-gather.7.cloned.1.call-update) | async-done | bytes 6815760 | tf_op jit(solution)/shard_map/all_gather | solution.py:67
  536.0 35.6 %fusion.10 = f32[512,4096]{1,0:T(8,128)} fusion(bf16[512,6656]{1,0:T(8,128)(2,1)} %all-gather.7.cloned.1.call-done, bf16[4096,6656]{1,0:T(8,128)(2,1)} %bitcast.20), kind=kOutput, calls=%fused_computation.29 | convolution fusion | flops 27917287424 | bytes 69730304 | tf_op jit(solution)/shard_map/dot_general | solution.py:71
  571.5 0.0 all-gather.11.cloned.1.call-start
  571.6 0.5 all-gather.11.cloned.1.call-update
  572.1 0.0 all-gather.9.cloned.1.call-start
  572.2 0.1 dynamic_slice.9
  572.3 0.1 dynamic_slice.11
  572.3 69.1 %reduce-scatter.5.cloned.1.call-done = f32[64,4096]{1,0:T(8,128)} async-done(((f32[512,4096]{1,0:T(8,128)}), f32[64,4096]{1,0:T(8,128)}) %reduce-scatter.5.cloned.1.call-update) | async-done | bytes 1048592 | tf_op jit(solution)/shard_map/reduce_scatter | solution.py:70
  641.4 1.5 multiply_reduce_fusion.1
  642.9 11.7 %psum.23 = f32[64]{0:T(128)S(1)} all-reduce(f32[64]{0:T(128)S(1)} %multiply_reduce_fusion.1), channel_id=1, replica_groups=mesh['batch'=4,'hidden'=2,'width'=4] {'width'}, use_global_device_ids=true, to_apply=%region_6.7 | all-reduce | flops 64 | bytes 512 | tf_op jit(solution)/shard_map/psum | solution.py:83
  654.6 1.0 select_convert_fusion
  655.7 12.7 %all-gather.11.cloned.1.call-done = bf16[4,512,640]{2,1,0:T(8,128)(2,1)} async-done(((bf16[1,512,640]{2,1,0:T(8,128)(2,1)}), bf16[4,512,640]{2,1,0:T(8,128)(2,1)}) %all-gather.11.cloned.1.call-update) | async-done | bytes 2621456 | tf_op jit(solution)/shard_map/all_gather | solution.py:88
  668.4 5.3 reshape.70
  673.7 33.7 %all-gather.9.cloned.1.call-done = bf16[512,4096]{1,0:T(8,128)(2,1)} async-done(((bf16[64,4096]{1,0:T(8,128)(2,1)}), bf16[512,4096]{1,0:T(8,128)(2,1)}) %all-gather.9.cloned.1.call-update) | async-done | bytes 4194320 | tf_op jit(solution)/shard_map/all_gather | solution.py:93
  707.4 22.7 %fusion.11 = f32[4096,2560]{0,1:T(8,128)} fusion(bf16[512,4096]{1,0:T(8,128)(2,1)} %all-gather.9.cloned.1.call-done, bf16[512,2560]{1,0:T(8,128)(2,1)} %reshape.70), kind=kOutput, calls=%fused_computation.30 | convolution fusion | flops 10737418240 | bytes 48758784 | tf_op jit(solution)/shard_map/dot_general | solution.py:91
  (18 shorter events, 0.1 us)
Async XLA Ops:
  7.2 78.6 %all-reduce.2.cloned.1.call-start = ((), (), s32[]{:S(2)}) async-start(), calls=%async_computation.2 | async-start | bytes 4194304 | tf_op jit(solution)/shard_map/psum | solution.py:27
  19.9 1.5 copy-start.3
  19.9 65.9 %copy-start.1 = (bf16[128,4096]{1,0:T(8,128)(2,1)S(1)}, bf16[128,4096]{1,0:T(8,128)(2,1)}, u32[]{:S(2)}) copy-start(bf16[128,4096]{1,0:T(8,128)(2,1)} %param.10) | copy-start | bytes 3145732
  19.9 120.3 %all-gather.5.cloned.1.call-start = ((), (), s32[]{:S(2)}) async-start(), calls=%async_computation.3 | async-start | bytes 5242880 | tf_op jit(solution)/shard_map/all_gather | solution.py:48
  102.8 302.9 %reduce-scatter.3.cloned.1.call-start = ((), (), s32[]{:S(2)}) async-start(), calls=%async_computation.4 | async-start | bytes 17039360 | tf_op jit(solution)/shard_map/reduce_scatter | solution.py:52
  179.1 226.6 %copy-start.2 = (bf16[128,3328]{1,0:T(8,128)(2,1)S(1)}, bf16[128,3328]{1,0:T(8,128)(2,1)}, u32[]{:S(2)}) copy-start(bf16[128,3328]{1,0:T(8,128)(2,1)} %param.15) | copy-start | bytes 2555908
  179.1 356.8 %all-gather.7.cloned.1.call-start = ((), (), s32[]{:S(2)}) async-start(), calls=%async_computation.5 | async-start | bytes 8519680 | tf_op jit(solution)/shard_map/all_gather | solution.py:67
  410.9 230.5 %reduce-scatter.5.cloned.1.call-start = ((), (), s32[]{:S(2)}) async-start(), calls=%async_computation.6 | async-start | bytes 9437184 | tf_op jit(solution)/shard_map/reduce_scatter | solution.py:70
  571.5 96.8 %all-gather.11.cloned.1.call-start = ((), (), s32[]{:S(2)}) async-start(), calls=%async_computation.8 | async-start | bytes 3276800 | tf_op jit(solution)/shard_map/all_gather | solution.py:88
  572.1 135.3 %all-gather.9.cloned.1.call-start = ((), (), s32[]{:S(2)}) async-start(), calls=%async_computation.7 | async-start | bytes 4718592 | tf_op jit(solution)/shard_map/all_gather | solution.py:93
  641.4 13.2 %copy-start = (f32[64,4096]{1,0:T(8,128)S(1)}, f32[64,4096]{1,0:T(8,128)}, u32[]{:S(2)}) copy-start(f32[64,4096]{1,0:T(8,128)} %reduce-scatter.5.cloned.1.call-done) | copy-start | bytes 3145732
Sparse Core Ops, SparseCore 0:
  20.0 65.6 all-reduce.1
  102.9 31.6 all-gather.4
  179.3 226.3 reduce-scatter.2
  411.0 124.9 all-gather.6
  571.7 69.6 reduce-scatter.4
  642.8 25.5 all-gather.10
  670.8 36.5 all-gather.8
where the time goes:
time: 737 us
  waiting for transfers between devices  532 us (72%)
  matrix products  108 us (15%)
  local copies, waits for them, and re-layouts  44.4 us (6%)
  blocking collectives  23.4 us (3%)
  between operations  15.5 us (2%)
  other arithmetic  13 us (2%)
    reduce_scatter x1, waiting for transfers between devices, on_device(): lax.psum_scatter(partial_pair, 'width', scatter_dimension=0, tiled=True)  226 us
    all_gather x1, waiting for transfers between devices, on_device(): all_pairs = lax.all_gather(grad_pair, 'width', axis=0, tiled=True)  125 us
    reduce_scatter x1, waiting for transfers between devices, on_device(): lax.psum_scatter(lax.dot_general(row_block, weights, (((1,), (1,)), ((),...  69.1 us
    psum x1, waiting for transfers between devices, on_device(): audio_part = lax.psum(partial_audio, 'hidden')  64.4 us
    dot_general x1, matrix products, on_device(): jnp.dot(lax.all_gather(normed, 'batch', axis=0, tiled=True), weights, pre...  38.9 us
    unnamed x9, local copies, waits for them, and re-layouts  37.4 us
    dot_general x1, matrix products, on_device(): lax.dot_general(row_block, weights, (((1,), (1,)), ((), ())), preferred_e...  35.6 us
    all_gather x1, waiting for transfers between devices, on_device(): lax.all_gather(audio_grad, ('batch', 'hidden'), axis=0, tiled=True)  33.7 us
  transfers between devices with their start and end apart: 7, of which 6 were waited for; matrix products, arithmetic and copies ran while one was open for 6% of the time, Pallas kernels for 0%

commit v1 on v0

v1 whole, which is shorter than its diff:
```python
import jax
import jax.numpy as jnp
from jax import lax
from jax.experimental import pallas as pl
from jax.experimental.pallas import tpu as pltpu
from jax.sharding import PartitionSpec as P


norm_eps = 1e-05
bf16, f16, f32 = jnp.bfloat16, jnp.float16, jnp.float32
audio_scale = 16.0
gate_scale = 32.0


def tied(value, *after):
    return lax.optimization_barrier((value,) + after)[0]


def bits(count):
    steps, step = [], 1
    while step < count:
        steps.append(step)
        step *= 2
    return steps


def swap(value, axis, step):
    return lax.ppermute(value, axis, [(i, i ^ step) for i in range(lax.axis_size(axis))])


def bit_of(axis, step):
    return (lax.axis_index(axis) // step) % 2


def put_pair(own, got, bit, dim):
    at = dim + 1
    shape = own.shape[:at] + (2,) + own.shape[at:]
    out = jnp.zeros(shape, own.dtype)
    out = lax.dynamic_update_slice_in_dim(out, jnp.expand_dims(own, at), bit, at)
    out = lax.dynamic_update_slice_in_dim(out, jnp.expand_dims(got, at), 1 - bit, at)
    return out.reshape(own.shape[:dim] + (-1,) + own.shape[at:])


def join(value, axis, step, dim):
    return put_pair(value, swap(value, axis, step), bit_of(axis, step), dim)


def spread(value, axis):
    out = value[None]
    for step in bits(lax.axis_size(axis))[::-1]:
        out = join(out, axis, step, 0)
    return out


def halve(value, axis, step, dim):
    bit = bit_of(axis, step)
    shape = value.shape
    pairs = value.reshape(shape[:dim] + (shape[dim] // 2, 2) + shape[dim + 1 :])
    kept = lax.dynamic_index_in_dim(pairs, bit, dim + 1, keepdims=False)
    sent = lax.dynamic_index_in_dim(pairs, 1 - bit, dim + 1, keepdims=False).astype(bf16)
    return kept + swap(sent, axis, step).astype(f32)


def quad_swap(value, axes, flips):
    sizes = [lax.axis_size(a) for a in axes]
    tops = [(n // 2) * f for n, f in zip(sizes, flips)]
    pairs = [
        (i * sizes[1] + j, (i ^ tops[0]) * sizes[1] + (j ^ tops[1]))
        for i in range(sizes[0])
        for j in range(sizes[1])
    ]
    return lax.ppermute(value, axes, pairs)


flips_of_quad = ((1, 0), (0, 1), (1, 1))


def top_bits(axes):
    return [bit_of(a, lax.axis_size(a) // 2) for a in axes]


def quad_sum(value, axes):
    x, y = top_bits(axes)

    def block(i, j):
        out = lax.dynamic_index_in_dim(value, i, 0, keepdims=False)
        return lax.dynamic_index_in_dim(out, j, 0, keepdims=False)

    total = block(x, y)
    for fx, fy in flips_of_quad:
        sent = block(x ^ fx, y ^ fy).astype(bf16)
        total = total + quad_swap(sent, axes, (fx, fy)).astype(f32)
    return total


def quad_spread(value, axes):
    x, y = top_bits(axes)
    out = jnp.zeros((2, 2) + value.shape, value.dtype)
    out = lax.dynamic_update_slice(out, value[None, None], (x, y, 0, 0))
    for fx, fy in flips_of_quad:
        got = quad_swap(value, axes, (fx, fy))
        out = lax.dynamic_update_slice(out, got[None, None], (x ^ fx, y ^ fy, 0, 0))
    return out


def line_sum(value, axis):
    n = lax.axis_size(axis)
    total = value
    for shift in range(1, n):
        total = total + lax.ppermute(value, axis, [(i, (i + shift) % n) for i in range(n)])
    return total


def right_of(n, tick, gather):
    return [(i, i + 1) for i in range(n - 1) if (i >= tick - 1 if gather else i < tick)]


def left_of(n, tick, gather):
    return [(n - 1 - i, n - 1 - j) for i, j in right_of(n, tick, gather)]


def line_scatter(parts, axis):
    n = lax.axis_size(axis)
    z = lax.axis_index(axis)

    def block(s):
        s = jnp.clip(s, 0, n - 1)
        blocks = [lax.dynamic_index_in_dim(p, s, 0, keepdims=False) for p in parts]
        return jnp.concatenate(blocks, axis=-1)

    right = left = None
    for tick in range(1, n):
        to_right, to_left = block(n + z - tick), block(z + tick - n)
        if tick > 1:
            to_right, to_left = to_right + right, to_left + left
        right = (to_right * gate_scale).astype(f16)
        left = (to_left * gate_scale).astype(f16)
        right = lax.ppermute(right, axis, right_of(n, tick, False))
        left = lax.ppermute(left, axis, left_of(n, tick, False))
        right, left = (v.astype(f32) * (1.0 / gate_scale) for v in (right, left))
    return block(z) + right + left


def back_kernel(grads_ref, gate_ref, up_ref, *refs):
    span = gate_ref.shape[1]
    dims = (((1,), (1,)), ((), ()))
    total = lax.dot_general(
        grads_ref[:, :span], gate_ref[...], dims, preferred_element_type=f32
    ) + lax.dot_general(grads_ref[:, span:], up_ref[...], dims, preferred_element_type=f32)
    if len(refs) == 2:
        total = total + refs[0][...]
    refs[-1][...] = total


def back(grads, w, c, chunks, so_far):
    rows, span = grads.shape[0], grads.shape[1] // 2
    width = w.shape[0]
    if span % 128:
        cols = jnp.concatenate(
            [w[:, (k * chunks + c) * span : (k * chunks + c + 1) * span] for k in range(2)], axis=1
        )
        total = lax.dot_general(
            grads, cols, (((1,), (1,)), ((), ())), preferred_element_type=f32
        )
        return total if so_far is None else total + so_far
    block = 512
    while width % block:
        block //= 2
    out_spec = pl.BlockSpec((rows, block), lambda i: (0, i))
    in_specs = [
        pl.BlockSpec((rows, 2 * span), lambda i: (0, 0)),
        pl.BlockSpec((block, span), lambda i: (i, c)),
        pl.BlockSpec((block, span), lambda i: (i, chunks + c)),
    ]
    args = [grads, w, w]
    if so_far is not None:
        in_specs.append(out_spec)
        args.append(so_far)
    return pl.pallas_call(
        back_kernel,
        grid=(width // block,),
        in_specs=in_specs,
        out_specs=out_spec,
        out_shape=jax.ShapeDtypeStruct((rows, width), f32),
        input_output_aliases={3: 0} if so_far is not None else {},
        compiler_params=pltpu.CompilerParams(vmem_limit_bytes=48 * 2**20),
        cost_estimate=pl.CostEstimate(
            flops=4 * rows * span * width,
            bytes_accessed=4 * width * span + 4 * rows * span + 4 * rows * width,
            transcendentals=0,
        ),
    )(*args)


def on_device(
    frames, adapter_weight, text_embed, audio_len, text_len, norm_gain, gate_up, cotangent
):
    frame_count, feat_here = frames.shape[1:]
    seq_len = frame_count // 4
    cap = seq_len // 2
    width_here = adapter_weight.shape[2]
    full_width = width_here * lax.axis_size("width")
    units = gate_up.shape[2]
    gain = norm_gain.astype(f32)[None, :]

    chunks = 2 if units % 256 == 0 else 1
    span = units // chunks

    places = jnp.arange(seq_len, dtype=jnp.int32)
    is_audio = (places[:cap] < audio_len[0])[:, None]
    is_text = (places < audio_len[0] + text_len[0])[:, None]
    text_rows = jnp.where(is_text, text_embed.astype(f32), 0.0)

    def inverse(squares):
        total = line_sum(squares, "width")
        return lax.rsqrt(total / full_width + norm_eps)[:, None]

    tail = text_rows[cap:]
    tail_squares = jnp.sum(tail * tail, axis=1)
    tail_norm = (tail * inverse(tail_squares) * gain).astype(bf16)
    tail_rows = spread(tail_norm, "batch")

    stacked = frames[0, : 4 * cap].reshape(cap, 4 * feat_here)
    kernel = adapter_weight.reshape(4 * feat_here, width_here)
    half = width_here // 2
    pieces = []
    for lo in (0, half):
        audio = jnp.dot(tied(stacked, tail_squares), kernel[:, lo : lo + half], preferred_element_type=f32)
        for step in bits(lax.axis_size("hidden")):
            got = swap((audio * audio_scale).astype(f16), "hidden", step)
            audio = audio + got.astype(f32) * (1.0 / audio_scale)
        pieces.append(audio)
    audio = jnp.concatenate(pieces, axis=1)
    head = jnp.where(is_audio, audio, text_rows[:cap])
    inv_rms = inverse(jnp.sum(head * head, axis=1))
    unit = head * inv_rms
    head_rows = spread((unit * gain).astype(bf16), "batch")
    count = head_rows.shape[0]
    n_head = count * cap

    rows = jnp.concatenate([head_rows, tail_rows], axis=0).reshape(2 * n_head, width_here)
    part = jnp.einsum("tf,fgh->gth", rows, gate_up, preferred_element_type=f32)
    part = lax.optimization_barrier(part)
    stack_all = spread(tied(stacked, part), "batch").reshape(n_head, 4 * feat_here)

    def chunk(c):
        return [part[k, :n_head, c * span : (c + 1) * span] for k in range(2)]

    def gates(summed):
        gate, up = jnp.split(summed, 2, axis=1)
        sig = jax.nn.sigmoid(gate)
        return gate, up, sig, gate * sig

    hidden_head, pairs, proj = [], [], 0.0
    for c in range(chunks):
        got = line_scatter([p.reshape(count, cap, span) for p in chunk(c)], "width")
        gate, up, sig, silu = gates(got)
        hidden_head.append((silu * up).astype(bf16))
        cot = cotangent[:cap, c * span : (c + 1) * span].astype(f32)
        slope = sig * (1.0 + gate * (1.0 - sig))
        grads = [(cot * up * slope).astype(bf16), (cot * silu).astype(bf16)]
        proj = proj + jnp.sum(gate * grads[0].astype(f32) + up * grads[1].astype(f32), axis=1)
        grads = jnp.concatenate(grads, axis=1)
        pairs.append(lax.all_gather(grads, "width", axis=0, tiled=True))

    last = pairs[-1]
    w = lax.optimization_barrier(tied(gate_up, grads).reshape(width_here, 2 * units))
    rest = lax.optimization_barrier((part[0, n_head:], part[1, n_head:], grads))[:2]
    rest = jnp.concatenate([p.astype(bf16) for p in rest], axis=1)
    proj = tied(proj, grads)

    lines = lax.axis_size("width")
    z = lax.axis_index("width")
    shared = jnp.zeros((lines, cap), f32)
    shared = lax.dynamic_update_slice_in_dim(shared, proj[None], z, 0)
    for shift in range(1, lines):
        ring = [(i, (i + shift) % lines) for i in range(lines)]
        got = lax.ppermute(proj, "width", ring)
        shared = lax.dynamic_update_slice_in_dim(shared, got[None], (z - shift) % lines, 0)
    for axis in ("batch", "hidden"):
        for step in bits(lax.axis_size(axis)):
            shared = shared + swap(shared, axis, step)

    pairs[-1], shared, rest = lax.optimization_barrier((pairs[-1], shared, rest))
    grad = None
    for c in range(chunks):
        grad = back(pairs[c], w, c, chunks, grad)

    groups = lax.axis_size("hidden")
    share = cap // groups
    grad = grad.reshape(count, groups, share, width_here)
    low = [("batch", step, 0) for step in bits(lax.axis_size("batch"))[:-1]]
    low += [("hidden", step, 1) for step in bits(groups)[:-1]]
    quad = ("batch", "hidden")
    for step in low:
        grad = halve(grad, *step)
    scaled = quad_sum(grad, quad) * gain
    start = lax.axis_index("hidden") * share
    unit = lax.dynamic_slice_in_dim(unit, start, share, 0)
    inv = lax.dynamic_slice_in_dim(inv_rms, start, share, 0)
    own = lax.axis_index("batch")
    proj = lax.dynamic_slice(shared, (own, start), (1, share))[0][:, None] / full_width
    grad = (scaled - unit * proj) * inv
    mine = (start + jnp.arange(share, dtype=jnp.int32) < audio_len[0])[:, None]
    grad = quad_spread(jnp.where(mine, grad, 0.0).astype(bf16), quad)
    for step in low[::-1]:
        grad = join(grad, *step)
    weight_grad = lax.dot_general(
        stack_all,
        grad.reshape(n_head, width_here),
        (((0,), (0,)), ((), ())),
        preferred_element_type=f32,
    )

    rest = lax.psum_scatter(tied(rest, last), "width", scatter_dimension=0, tiled=True)
    rest, weight_grad = lax.optimization_barrier((rest, weight_grad))
    _, up, _, silu = gates(rest.astype(f32))
    hidden_tail = (silu * up).astype(bf16)
    hidden = jnp.concatenate([jnp.concatenate(hidden_head, axis=1), hidden_tail], axis=0)
    return (hidden, weight_grad.reshape(4, feat_here, width_here))


def solution(mesh):
    return jax.shard_map(
        on_device,
        mesh=mesh,
        in_specs=(
            P("batch", None, "hidden"),
            P(None, "hidden", "width"),
            P("batch", "width"),
            P("batch"),
            P("batch"),
            P("width"),
            P("width", None, ("batch", "hidden")),
            P("width", ("batch", "hidden")),
        ),
        out_specs=(P("width", ("batch", "hidden")), P(None, "hidden", "width")),
        check_vma=False,
    )
```

time: 737 us -> 388 us (0.53)
  waiting for transfers between devices: 532 us -> 141 us
  starting transfers between devices: 0.47 us -> 57 us
  matrix products: 108 us -> 73.4 us
  Pallas kernels: 0 us -> 28.6 us
  blocking collectives: 23.4 us -> 0 us
  local copies, waits for them, and re-layouts: 44.4 us -> 53.3 us
    reduce_scatter x2 -> x1, waiting for transfers between devices: 295 us -> 27.8 us  [on_device(): lax.psum_scatter(tied(rest, last), 'width', scatter_dimension=0, tiled=True)]
    all_gather x4 -> x2, waiting for transfers between devices: 171 us -> 24.6 us  [on_device(): pairs.append(lax.all_gather(grads, 'width', axis=0, tiled=True))]
    ppermute x0 -> x40, waiting for transfers between devices: none -> 88.8 us  [the longest x13 31.4 us: swap(): lax.ppermute(value, axis, [(i, i ^ step) for i in range(lax.axis_size(axi...]
    psum x1 -> x0, waiting for transfers between devices: 64.4 us -> none  [on_device(): audio_part = lax.psum(partial_audio, 'hidden')]
    ppermute x0 -> x40, starting transfers between devices: none -> 56.9 us  [the longest x6 20.5 us: line_scatter(): right = lax.ppermute(right, axis, right_of(n, tick, False))]
    dot_general x4, matrix products: 108 us -> 73.4 us  [the longest x1 42.7 us: on_device(): part = jnp.einsum('tf,fgh->gth', rows, gate_up, preferred_element_type=f32)]
    pallas_call x0 -> x2, Pallas kernels: none -> 28.6 us  [back(): pl.pallas_call(back_kernel, grid=(width // block,), in_specs=in_specs, ou...]
    psum x2 -> x0, blocking collectives: 23.4 us -> none  [the longest x1 11.7 us: on_device(): proj_stat = lax.psum(jnp.sum(unit_share * scaled_grad, axis=1), 'width') / D]
  transfers between devices with their start and end apart: 7 -> 43, of which waited for: 6 -> 24; matrix products, arithmetic and copies ran while one was open for 6% -> 22% of each run, Pallas kernels for 0% -> 0%
where the time goes in v1:
time: 388 us
  waiting for transfers between devices  141 us (36%)
  matrix products  73.4 us (19%)
  starting transfers between devices  57 us (15%)
  local copies, waits for them, and re-layouts  53.3 us (14%)
  Pallas kernels  28.6 us (7%)
  other arithmetic  18 us (5%)
  between operations  16 us (4%)
    dot_general x1, matrix products, on_device(): part = jnp.einsum('tf,fgh->gth', rows, gate_up, preferred_element_type=f32)  42.7 us
    unnamed x27, local copies, waits for them, and re-layouts  40.6 us
    ppermute x13, waiting for transfers between devices, swap(): lax.ppermute(value, axis, [(i, i ^ step) for i in range(lax.axis_size(axi...  31.4 us
    ppermute x6, waiting for transfers between devices, line_scatter(): right = lax.ppermute(right, axis, right_of(n, tick, False))  29.1 us
    pallas_call x2, Pallas kernels, back(): pl.pallas_call(back_kernel, grid=(width // block,), in_specs=in_specs, ou...  28.6 us
    reduce_scatter x1, waiting for transfers between devices, on_device(): lax.psum_scatter(tied(rest, last), 'width', scatter_dimension=0, tiled=True)  27.8 us
    all_gather x2, waiting for transfers between devices, on_device(): pairs.append(lax.all_gather(grads, 'width', axis=0, tiled=True))  24.6 us
    ppermute x6, waiting for transfers between devices, quad_swap(): return lax.ppermute(value, axes, pairs)  22.2 us
  transfers between devices with their start and end apart: 43, of which 24 were waited for; matrix products, arithmetic and copies ran while one was open for 22% of the time, Pallas kernels for 0%

profile of v1, /device:TPU:0, one launch (start us, length us, event | category | flops | bytes accessed | tf_op | source)
XLA Modules:
  0.0 387.7 jit_solution(12673073720487066938)
XLA Ops:
  10.2 5.1 %collective-permute-start.9 = (f32[64]{0:T(128)S(1)}, f32[64]{0:T(128)S(1)}, u32[]{:S(2)}, u32[]{:S(2)}) collective-permute-start(f32[64]{0:T(128)S(1)} %multiply_reduce_fusion.1), channel_id=1, source_target_pairs={{0,3},{1,0},{2,1},{3,2},{4,7},{5,4},{6,5},{7,6},{8,11},{9,8},{10,9... | collective-permute-start | bytes 776 | tf_op jit(solution)/shard_map/ppermute | solution.py:110
  16.6 6.7 %multiply_convert_fusion.2 = (f16[64,2048]{1,0:T(8,128)(2,1)}, f32[64,2048]{1,0:T(8,128)S(1)}) fusion(bf16[64,2560]{1,0:T(8,128)(2,1)S(1)} %reshape_squeeze.15, bf16[2560,4096]{1,0:T(8,128)(2,1)} %bitcast.199), kind=kOutput, calls=%fused_computation.88 | convolution fusion | flops 671350784 | bytes 11599872 | tf_op jit(solution)/shard_map/dot_general | solution.py:228
  24.9 6.6 %multiply_convert_fusion.3 = (f16[64,2048]{1,0:T(8,128)(2,1)}, f32[64,2048]{1,0:T(8,128)S(1)}) fusion(bf16[64,2560]{1,0:T(8,128)(2,1)S(1)} %reshape_squeeze.15, bf16[2560,4096]{1,0:T(8,128)(2,1)} %bitcast.200), kind=kOutput, calls=%fused_computation.90 | convolution fusion | flops 671350784 | bytes 11599872 | tf_op jit(solution)/shard_map/dot_general | solution.py:228
  33.1 5.5 %collective-permute-done = f16[64,2048]{1,0:T(8,128)(2,1)S(1)} collective-permute-done((f16[64,2048]{1,0:T(8,128)(2,1)}, f16[64,2048]{1,0:T(8,128)(2,1)S(1)}, u32[]{:S(2)}, u32[]{:S(2)}) %collective-permute-start) | collective-permute-done | bytes 262176 | tf_op jit(solution)/shard_map/ppermute | solution.py:28
  39.0 3.1 collective-permute-start.4
  43.6 3.1 collective-permute-done.3
  51.1 12.6 %collective-permute-done.10 = bf16[1,64,4096]{2,1,0:T(8,128)(2,1)S(1)} collective-permute-done((bf16[1,64,4096]{2,1,0:T(8,128)(2,1)S(1)}, bf16[1,64,4096]{2,1,0:T(8,128)(2,1)S(1)}, u32[]{:S(2)}, u32[]{:S(2)}) %collective-permute-start.10) | collective-permute-done | bytes 524320 | tf_op jit(solution)/shard_map/ppermute | solution.py:28
  63.8 6.3 %collective-permute-done.5 = bf16[1,64,4096]{2,1,0:T(8,128)(2,1)S(1)} collective-permute-done((bf16[1,64,4096]{2,1,0:T(8,128)(2,1)S(1)}, bf16[1,64,4096]{2,1,0:T(8,128)(2,1)S(1)}, u32[]{:S(2)}, u32[]{:S(2)}) %collective-permute-start.5) | collective-permute-done | bytes 524320 | tf_op jit(solution)/shard_map/ppermute | solution.py:28
  75.4 42.7 %fusion.6 = f32[2,512,3328]{2,1,0:T(8,128)} fusion(bf16[512,4096,1]{1,0,2:T(8,128)(2,1)} %bitcast.192, bf16[4096,2,3328]{2,1,0:T(2,128)(2,1)} %param.14), kind=kOutput, calls=%fused_computation.6 | convolution fusion | flops 27917287424 | bytes 72351744 | tf_op jit(solution)/shard_map/tf,fgh->gth/dot_general | solution.py:242
  118.0 3.4 fusion.58
  127.9 6.4 %collective-permute-done.12 = f16[64,3328]{1,0:T(8,128)(2,1)S(1)} collective-permute-done((f16[64,3328]{1,0:T(8,128)(2,1)S(1)}, f16[64,3328]{1,0:T(8,128)(2,1)S(1)}, u32[]{:S(2)}, u32[]{:S(2)}) %collective-permute-start.12) | collective-permute-done | bytes 426016 | tf_op jit(solution)/shard_map/ppermute | solution.py:138
  134.5 4.4 %collective-permute-start.13 = (f16[64,3328]{1,0:T(8,128)(2,1)S(1)}, f16[64,3328]{1,0:T(8,128)(2,1)S(1)}, u32[]{:S(2)}, u32[]{:S(2)}) collective-permute-start(f16[64,3328]{1,0:T(8,128)(2,1)S(1)} %fusion.15), channel_id=1, source_target_pairs={{0,1},{1,2},{4,5},{5,6},{8,9},{9,10},{12,13},{13,14},{16,17},{17,1... | collective-permute-start | bytes 1277960 | tf_op jit(solution)/shard_map/ppermute | solution.py:138
  139.8 3.7 collective-permute-done.18
  143.6 4.4 %collective-permute-start.19 = (f16[64,3328]{1,0:T(8,128)(2,1)S(1)}, f16[64,3328]{1,0:T(8,128)(2,1)S(1)}, u32[]{:S(2)}, u32[]{:S(2)}) collective-permute-start(f16[64,3328]{1,0:T(8,128)(2,1)S(1)} %fusion.26), channel_id=1, source_target_pairs={{0,1},{1,2},{4,5},{5,6},{8,9},{9,10},{12,13},{13,14},{16,17},{17,1... | collective-permute-start | bytes 1277960 | tf_op jit(solution)/shard_map/ppermute | solution.py:138
  149.5 3.1 collective-permute-done.13
  152.7 4.4 %collective-permute-start.14 = (f16[64,3328]{1,0:T(8,128)(2,1)S(1)}, f16[64,3328]{1,0:T(8,128)(2,1)S(1)}, u32[]{:S(2)}, u32[]{:S(2)}) collective-permute-start(f16[64,3328]{1,0:T(8,128)(2,1)S(1)} %fusion.13), channel_id=1, source_target_pairs={{0,1},{1,2},{2,3},{4,5},{5,6},{6,7},{8,9},{9,10},{10,11},{12,13},{... | collective-permute-start | bytes 1277960 | tf_op jit(solution)/shard_map/ppermute | solution.py:138
  158.6 3.1 collective-permute-done.19
  161.9 4.4 %collective-permute-start.20 = (f16[64,3328]{1,0:T(8,128)(2,1)S(1)}, f16[64,3328]{1,0:T(8,128)(2,1)S(1)}, u32[]{:S(2)}, u32[]{:S(2)}) collective-permute-start(f16[64,3328]{1,0:T(8,128)(2,1)S(1)} %fusion.24), channel_id=1, source_target_pairs={{0,1},{1,2},{2,3},{4,5},{5,6},{6,7},{8,9},{9,10},{10,11},{12,13},{... | collective-permute-start | bytes 1277960 | tf_op jit(solution)/shard_map/ppermute | solution.py:138
  166.3 4.5 %collective-permute-done.14 = f16[64,3328]{1,0:T(8,128)(2,1)S(1)} collective-permute-done((f16[64,3328]{1,0:T(8,128)(2,1)S(1)}, f16[64,3328]{1,0:T(8,128)(2,1)S(1)}, u32[]{:S(2)}, u32[]{:S(2)}) %collective-permute-start.14) | collective-permute-done | bytes 426016 | tf_op jit(solution)/shard_map/ppermute | solution.py:138
  171.1 8.3 %collective-permute-done.20 = f16[64,3328]{1,0:T(8,128)(2,1)S(1)} collective-permute-done((f16[64,3328]{1,0:T(8,128)(2,1)S(1)}, f16[64,3328]{1,0:T(8,128)(2,1)S(1)}, u32[]{:S(2)}, u32[]{:S(2)}) %collective-permute-start.20) | collective-permute-done | bytes 426016 | tf_op jit(solution)/shard_map/ppermute | solution.py:138
  184.9 2.8 collective-permute-start.26
  192.0 3.3 slice_bitcast_fusion
  197.9 36.9 %copy.22 = bf16[512,8,2,3328]{3,1,2,0:T(8,128)(2,1)} copy(bf16[512,8,2,3328]{3,2,1,0:T(2,128)(2,1)} %bitcast.180) | data formatting | bytes 109051904
  234.8 24.6 %all-gather.5.cloned.1.call-done.grads_ref = bf16[256,3328]{1,0:T(8,128)(2,1)} async-done(((bf16[64,3328]{1,0:T(8,128)(2,1)}), bf16[256,3328]{1,0:T(8,128)(2,1)}) %all-gather.5.cloned.1.call-update) | async-done | bytes 1703952 | tf_op jit(solution)/shard_map/all_gather | solution.py:264
  260.9 14.3 %shard_map.95.refs_0_ = f32[256,4096]{1,0:T(8,128)S(1)} custom-call(bf16[256,3328]{1,0:T(8,128)(2,1)S(1)} %copy-done.2, bf16[4096,6656]{1,0:T(8,128)(2,1)} %bitcast.176, bf16[4096,6656]{1,0:T(8,128)(2,1)} %bitcast.177), custom_call_target="tpu_custom_call" | custom-call | flops 6979321856 | bytes 33161216 | tf_op jit(solution)/shard_map/pallas_call | solution.py:179
  275.2 14.3 %shard_map.96 = f32[256,4096]{1,0:T(8,128)S(1)} custom-call(bf16[256,3328]{1,0:T(8,128)(2,1)S(1)} %copy-done.1, bf16[4096,6656]{1,0:T(8,128)(2,1)} %bitcast.178, bf16[4096,6656]{1,0:T(8,128)(2,1)} %bitcast.179, f32[256,4096]{1,0:T(8,128)S(1)} %shard_map.95.refs_0_), custom_call_target="tpu_custom_call", output_to_operand_aliasing={{}: (3, {})} | custom-call | flops 6979321856 | bytes 33161216 | tf_op jit(solution)/shard_map/pallas_call | solution.py:179
  302.6 6.5 %collective-permute-done.35 = bf16[32,4096]{1,0:T(8,128)(2,1)S(1)} collective-permute-done((bf16[32,4096]{1,0:T(8,128)(2,1)S(1)}, bf16[32,4096]{1,0:T(8,128)(2,1)S(1)}, u32[]{:S(2)}, u32[]{:S(2)}) %collective-permute-start.35) | collective-permute-done | bytes 262176 | tf_op jit(solution)/shard_map/ppermute | solution.py:72
  309.0 3.8 collective-permute-done.34
  318.1 5.7 %collective-permute-done.36 = bf16[32,4096]{1,0:T(8,128)(2,1)} collective-permute-done((bf16[32,4096]{1,0:T(8,128)(2,1)}, bf16[32,4096]{1,0:T(8,128)(2,1)}, u32[]{:S(2)}, u32[]{:S(2)}) %collective-permute-start.36) | collective-permute-done | bytes 262176 | tf_op jit(solution)/shard_map/ppermute | solution.py:72
  324.7 5.9 %collective-permute-done.37 = bf16[32,4096]{1,0:T(8,128)(2,1)S(1)} collective-permute-done((bf16[32,4096]{1,0:T(8,128)(2,1)}, bf16[32,4096]{1,0:T(8,128)(2,1)S(1)}, u32[]{:S(2)}, u32[]{:S(2)}) %collective-permute-start.37) | collective-permute-done | bytes 262176 | tf_op jit(solution)/shard_map/ppermute | solution.py:72
  333.5 17.4 %fusion.59 = f32[2560,4096]{1,0:T(8,128)} fusion(bf16[256,2560]{1,0:T(8,128)(2,1)S(1)} %bitcast.189, bf16[256,4096]{1,0:T(8,128)(2,1)S(1)} %bitcast.186), kind=kOutput, calls=%fused_computation.153 | convolution fusion | flops 5368709120 | bytes 45350912 | tf_op jit(solution)/shard_map/dot_general | solution.py:308
  350.9 27.8 %reduce-scatter.2.cloned.1.call-done = bf16[64,6656]{1,0:T(8,128)(2,1)} async-done(((bf16[256,6656]{1,0:T(8,128)(2,1)}), bf16[64,6656]{1,0:T(8,128)(2,1)}) %reduce-scatter.2.cloned.1.call-update) | async-done | bytes 851984 | tf_op jit(solution)/shard_map/reduce_scatter | solution.py:315
  (174 shorter events, 66.5 us)
Async XLA Ops:
  7.2 227.6 %all-gather.3.cloned.1.call-start = ((), (), s32[]{:S(2)}) async-start(), calls=%async_computation.1 | async-start | bytes 2129920 | tf_op jit(solution)/shard_map/all_gather | solution.py:264
  10.2 21.8 %collective-permute-start.9 = (f32[64]{0:T(128)S(1)}, f32[64]{0:T(128)S(1)}, u32[]{:S(2)}, u32[]{:S(2)}) collective-permute-start(f32[64]{0:T(128)S(1)} %multiply_reduce_fusion.1), channel_id=1, source_target_pairs={{0,3},{1,0},{2,1},{3,2},{4,7},{5,4},{6,5},{7,6},{8,11},{9,8},{10,9... | collective-permute-start | bytes 776 | tf_op jit(solution)/shard_map/ppermute | solution.py:110
  15.4 16.7 %collective-permute-start.8 = (f32[64]{0:T(128)S(1)}, f32[64]{0:T(128)S(1)}, u32[]{:S(2)}, u32[]{:S(2)}) collective-permute-start(f32[64]{0:T(128)S(1)} %multiply_reduce_fusion.1), channel_id=1, source_target_pairs={{0,2},{1,3},{2,0},{3,1},{4,6},{5,7},{6,4},{7,5},{8,10},{9,11},{10,... | collective-permute-start | bytes 776 | tf_op jit(solution)/shard_map/ppermute | solution.py:110
  15.4 16.7 %collective-permute-start.7 = (f32[64]{0:T(128)S(1)}, f32[64]{0:T(128)S(1)}, u32[]{:S(2)}, u32[]{:S(2)}) collective-permute-start(f32[64]{0:T(128)S(1)} %multiply_reduce_fusion.1), channel_id=1, source_target_pairs={{0,1},{1,2},{2,3},{3,0},{4,5},{5,6},{6,7},{7,4},{8,9},{9,10},{10,1... | collective-permute-start | bytes 776 | tf_op jit(solution)/shard_map/ppermute | solution.py:110
  23.3 8.8 %collective-permute-start.1 = (f16[64,2048]{1,0:T(8,128)(2,1)}, f16[64,2048]{1,0:T(8,128)(2,1)}, u32[]{:S(2)}, u32[]{:S(2)}) collective-permute-start(f16[64,2048]{1,0:T(8,128)(2,1)} %get-tuple-element.79), channel_id=1, source_target_pairs={{0,4},{4,0},{1,5},{5,1},{2,6},{6,2},{3,7},{7,3},{8,12},{12,8},{9,1... | collective-permute-start | bytes 786440 | tf_op jit(solution)/shard_map/ppermute | solution.py:28
  31.5 7.1 %collective-permute-start = (f16[64,2048]{1,0:T(8,128)(2,1)}, f16[64,2048]{1,0:T(8,128)(2,1)S(1)}, u32[]{:S(2)}, u32[]{:S(2)}) collective-permute-start(f16[64,2048]{1,0:T(8,128)(2,1)} %get-tuple-element.81), channel_id=1, source_target_pairs={{0,4},{4,0},{1,5},{5,1},{2,6},{6,2},{3,7},{7,3},{8,12},{12,8},{9,1... | collective-permute-start | bytes 786440 | tf_op jit(solution)/shard_map/ppermute | solution.py:28
  48.9 14.8 %collective-permute-start.10 = (bf16[1,64,4096]{2,1,0:T(8,128)(2,1)S(1)}, bf16[1,64,4096]{2,1,0:T(8,128)(2,1)S(1)}, u32[]{:S(2)}, u32[]{:S(2)}) collective-permute-start(bf16[1,64,4096]{2,1,0:T(8,128)(2,1)S(1)} %get-tuple-element.42), channel_id=1, source_target_pairs={{0,16},{8,24},{16,0},{24,8},{1,17},{9,25},{17,1},{25,9},{2,18},{10... | collective-permute-start | bytes 1572872 | tf_op jit(solution)/shard_map/ppermute | solution.py:28
  50.4 19.7 %collective-permute-start.5 = (bf16[1,64,4096]{2,1,0:T(8,128)(2,1)S(1)}, bf16[1,64,4096]{2,1,0:T(8,128)(2,1)S(1)}, u32[]{:S(2)}, u32[]{:S(2)}) collective-permute-start(bf16[1,64,4096]{2,1,0:T(8,128)(2,1)S(1)} %get-tuple-element.34), channel_id=1, source_target_pairs={{0,16},{8,24},{16,0},{24,8},{1,17},{9,25},{17,1},{25,9},{2,18},{10... | collective-permute-start | bytes 1572872 | tf_op jit(solution)/shard_map/ppermute | solution.py:28
  63.8 7.4 %collective-permute-start.11 = (bf16[2,64,4096]{2,1,0:T(8,128)(2,1)S(1)}, bf16[2,64,4096]{2,1,0:T(8,128)(2,1)S(1)}, u32[]{:S(2)}, u32[]{:S(2)}) collective-permute-start(bf16[2,64,4096]{2,1,0:T(8,128)(2,1)S(1)} %bitcast.190), channel_id=1, source_target_pairs={{0,8},{8,0},{16,24},{24,16},{1,9},{9,1},{17,25},{25,17},{2,10},{10... | collective-permute-start | bytes 3145736 | tf_op jit(solution)/shard_map/ppermute | solution.py:28
  122.8 11.5 %collective-permute-start.12 = (f16[64,3328]{1,0:T(8,128)(2,1)S(1)}, f16[64,3328]{1,0:T(8,128)(2,1)S(1)}, u32[]{:S(2)}, u32[]{:S(2)}) collective-permute-start(f16[64,3328]{1,0:T(8,128)(2,1)S(1)} %fusion.16), channel_id=1, source_target_pairs={{0,1},{4,5},{8,9},{12,13},{16,17},{20,21},{24,25},{28,29}} | collective-permute-start | bytes 1277960 | tf_op jit(solution)/shard_map/ppermute | solution.py:138
  124.9 14.0 %collective-permute-start.21 = (f16[64,3328]{1,0:T(8,128)(2,1)S(1)}, f16[64,3328]{1,0:T(8,128)(2,1)S(1)}, u32[]{:S(2)}, u32[]{:S(2)}) collective-permute-start(f16[64,3328]{1,0:T(8,128)(2,1)S(1)} %fusion.32), channel_id=1, source_target_pairs={{3,2},{7,6},{11,10},{15,14},{19,18},{23,22},{27,26},{31,30}} | collective-permute-start | bytes 1277960 | tf_op jit(solution)/shard_map/ppermute | solution.py:139
  125.7 17.8 %collective-permute-start.18 = (f16[64,3328]{1,0:T(8,128)(2,1)S(1)}, f16[64,3328]{1,0:T(8,128)(2,1)S(1)}, u32[]{:S(2)}, u32[]{:S(2)}) collective-permute-start(f16[64,3328]{1,0:T(8,128)(2,1)S(1)} %fusion.27), channel_id=1, source_target_pairs={{0,1},{4,5},{8,9},{12,13},{16,17},{20,21},{24,25},{28,29}} | collective-permute-start | bytes 1277960 | tf_op jit(solution)/shard_map/ppermute | solution.py:138
  127.2 20.9 %collective-permute-start.16 = (f16[64,3328]{1,0:T(8,128)(2,1)S(1)}, f16[64,3328]{1,0:T(8,128)(2,1)S(1)}, u32[]{:S(2)}, u32[]{:S(2)}) collective-permute-start(f16[64,3328]{1,0:T(8,128)(2,1)S(1)} %fusion.20), channel_id=1, source_target_pairs={{3,2},{2,1},{7,6},{6,5},{11,10},{10,9},{15,14},{14,13},{19,18},{18... | collective-permute-start | bytes 1277960 | tf_op jit(solution)/shard_map/ppermute | solution.py:139
  134.5 18.1 %collective-permute-start.13 = (f16[64,3328]{1,0:T(8,128)(2,1)S(1)}, f16[64,3328]{1,0:T(8,128)(2,1)S(1)}, u32[]{:S(2)}, u32[]{:S(2)}) collective-permute-start(f16[64,3328]{1,0:T(8,128)(2,1)S(1)} %fusion.15), channel_id=1, source_target_pairs={{0,1},{1,2},{4,5},{5,6},{8,9},{9,10},{12,13},{13,14},{16,17},{17,1... | collective-permute-start | bytes 1277960 | tf_op jit(solution)/shard_map/ppermute | solution.py:138
  139.1 18.1 %collective-permute-start.22 = (f16[64,3328]{1,0:T(8,128)(2,1)S(1)}, f16[64,3328]{1,0:T(8,128)(2,1)S(1)}, u32[]{:S(2)}, u32[]{:S(2)}) collective-permute-start(f16[64,3328]{1,0:T(8,128)(2,1)S(1)} %fusion.31), channel_id=1, source_target_pairs={{3,2},{2,1},{7,6},{6,5},{11,10},{10,9},{15,14},{14,13},{19,18},{18... | collective-permute-start | bytes 1277960 | tf_op jit(solution)/shard_map/ppermute | solution.py:139
  143.6 18.1 %collective-permute-start.19 = (f16[64,3328]{1,0:T(8,128)(2,1)S(1)}, f16[64,3328]{1,0:T(8,128)(2,1)S(1)}, u32[]{:S(2)}, u32[]{:S(2)}) collective-permute-start(f16[64,3328]{1,0:T(8,128)(2,1)S(1)} %fusion.26), channel_id=1, source_target_pairs={{0,1},{1,2},{4,5},{5,6},{8,9},{9,10},{12,13},{13,14},{16,17},{17,1... | collective-permute-start | bytes 1277960 | tf_op jit(solution)/shard_map/ppermute | solution.py:138
  148.2 18.1 %collective-permute-start.17 = (f16[64,3328]{1,0:T(8,128)(2,1)S(1)}, f16[64,3328]{1,0:T(8,128)(2,1)S(1)}, u32[]{:S(2)}, u32[]{:S(2)}) collective-permute-start(f16[64,3328]{1,0:T(8,128)(2,1)S(1)} %fusion.18), channel_id=1, source_target_pairs={{3,2},{2,1},{1,0},{7,6},{6,5},{5,4},{11,10},{10,9},{9,8},{15,14},{... | collective-permute-start | bytes 1277960 | tf_op jit(solution)/shard_map/ppermute | solution.py:139
  152.7 18.1 %collective-permute-start.14 = (f16[64,3328]{1,0:T(8,128)(2,1)S(1)}, f16[64,3328]{1,0:T(8,128)(2,1)S(1)}, u32[]{:S(2)}, u32[]{:S(2)}) collective-permute-start(f16[64,3328]{1,0:T(8,128)(2,1)S(1)} %fusion.13), channel_id=1, source_target_pairs={{0,1},{1,2},{2,3},{4,5},{5,6},{6,7},{8,9},{9,10},{10,11},{12,13},{... | collective-permute-start | bytes 1277960 | tf_op jit(solution)/shard_map/ppermute | solution.py:138
  157.3 13.8 %collective-permute-start.23 = (f16[64,3328]{1,0:T(8,128)(2,1)S(1)}, f16[64,3328]{1,0:T(8,128)(2,1)S(1)}, u32[]{:S(2)}, u32[]{:S(2)}) collective-permute-start(f16[64,3328]{1,0:T(8,128)(2,1)S(1)} %fusion.29), channel_id=1, source_target_pairs={{3,2},{2,1},{1,0},{7,6},{6,5},{5,4},{11,10},{10,9},{9,8},{15,14},{... | collective-permute-start | bytes 1277960 | tf_op jit(solution)/shard_map/ppermute | solution.py:139
  161.9 17.5 %collective-permute-start.20 = (f16[64,3328]{1,0:T(8,128)(2,1)S(1)}, f16[64,3328]{1,0:T(8,128)(2,1)S(1)}, u32[]{:S(2)}, u32[]{:S(2)}) collective-permute-start(f16[64,3328]{1,0:T(8,128)(2,1)S(1)} %fusion.24), channel_id=1, source_target_pairs={{0,1},{1,2},{2,3},{4,5},{5,6},{6,7},{8,9},{9,10},{10,11},{12,13},{... | collective-permute-start | bytes 1277960 | tf_op jit(solution)/shard_map/ppermute | solution.py:138
  181.2 78.2 %all-gather.5.cloned.1.call-start = ((), (), s32[]{:S(2)}) async-start(), calls=%async_computation.3 | async-start | bytes 2129920 | tf_op jit(solution)/shard_map/all_gather | solution.py:264
  182.1 196.7 %reduce-scatter.2.cloned.1.call-start = ((), (), s32[]{:S(2)}) async-start(), calls=%async_computation.2 | async-start | bytes 4259840 | tf_op jit(solution)/shard_map/reduce_scatter | solution.py:315
  182.2 5.6 %collective-permute-start.24 = (f32[64]{0:T(128)S(1)}, f32[64]{0:T(128)S(1)}, u32[]{:S(2)}, u32[]{:S(2)}) collective-permute-start(f32[64]{0:T(128)S(1)} %add.341), channel_id=1, source_target_pairs={{0,1},{1,2},{2,3},{3,0},{4,5},{5,6},{6,7},{7,4},{8,9},{9,10},{10,1... | collective-permute-start | bytes 776 | tf_op jit(solution)/shard_map/ppermute | solution.py:278
  195.3 39.4 %collective-permute-start.29 = (f32[4,64]{1,0:T(4,128)S(1)}, f32[4,64]{1,0:T(4,128)S(1)}, u32[]{:S(2)}, u32[]{:S(2)}) collective-permute-start(f32[4,64]{1,0:T(4,128)S(1)} %add.350), channel_id=1, source_target_pairs={{0,4},{4,0},{1,5},{5,1},{2,6},{6,2},{3,7},{7,3},{8,12},{12,8},{9,1... | collective-permute-start | bytes 3080 | tf_op jit(solution)/shard_map/ppermute | solution.py:28
  291.9 10.6 %collective-permute-start.30 = (bf16[1,64,2560]{2,1,0:T(8,128)(2,1)S(1)}, bf16[1,64,2560]{2,1,0:T(8,128)(2,1)S(1)}, u32[]{:S(2)}, u32[]{:S(2)}) collective-permute-start(bf16[1,64,2560]{2,1,0:T(8,128)(2,1)S(1)} %bitcast.194), channel_id=1, source_target_pairs={{0,16},{8,24},{16,0},{24,8},{1,17},{9,25},{17,1},{25,9},{2,18},{10... | collective-permute-start | bytes 983048 | tf_op jit(solution)/shard_map/ppermute | solution.py:28
  296.8 12.3 %collective-permute-start.35 = (bf16[32,4096]{1,0:T(8,128)(2,1)S(1)}, bf16[32,4096]{1,0:T(8,128)(2,1)S(1)}, u32[]{:S(2)}, u32[]{:S(2)}) collective-permute-start(bf16[32,4096]{1,0:T(8,128)(2,1)S(1)} %get-tuple-element.44), channel_id=1, source_target_pairs={{0,20},{4,16},{8,28},{12,24},{16,4},{20,0},{24,12},{28,8},{1,21},{... | collective-permute-start | bytes 786440 | tf_op jit(solution)/shard_map/ppermute | solution.py:72
  299.2 13.7 %collective-permute-start.34 = (bf16[32,4096]{1,0:T(8,128)(2,1)S(1)}, bf16[32,4096]{1,0:T(8,128)(2,1)S(1)}, u32[]{:S(2)}, u32[]{:S(2)}) collective-permute-start(bf16[32,4096]{1,0:T(8,128)(2,1)S(1)} %get-tuple-element.45), channel_id=1, source_target_pairs={{0,4},{4,0},{8,12},{12,8},{16,20},{20,16},{24,28},{28,24},{1,5},{5... | collective-permute-start | bytes 786440 | tf_op jit(solution)/shard_map/ppermute | solution.py:72
  299.7 13.5 %collective-permute-start.33 = (bf16[32,4096]{1,0:T(8,128)(2,1)S(1)}, bf16[32,4096]{1,0:T(8,128)(2,1)S(1)}, u32[]{:S(2)}, u32[]{:S(2)}) collective-permute-start(bf16[32,4096]{1,0:T(8,128)(2,1)S(1)} %get-tuple-element.43), channel_id=1, source_target_pairs={{0,16},{4,20},{8,24},{12,28},{16,0},{20,4},{24,8},{28,12},{1,17},{... | collective-permute-start | bytes 786440 | tf_op jit(solution)/shard_map/ppermute | solution.py:72
  314.3 9.5 %collective-permute-start.36 = (bf16[32,4096]{1,0:T(8,128)(2,1)}, bf16[32,4096]{1,0:T(8,128)(2,1)}, u32[]{:S(2)}, u32[]{:S(2)}) collective-permute-start(bf16[32,4096]{1,0:T(8,128)(2,1)} %get-tuple-element.27), channel_id=1, source_target_pairs={{0,16},{4,20},{8,24},{12,28},{16,0},{20,4},{24,8},{28,12},{1,17},{... | collective-permute-start | bytes 786440 | tf_op jit(solution)/shard_map/ppermute | solution.py:72
  315.9 14.9 %collective-permute-start.31 = (bf16[2,64,2560]{2,1,0:T(8,128)(2,1)S(1)}, bf16[2,64,2560]{2,1,0:T(8,128)(2,1)}, u32[]{:S(2)}, u32[]{:S(2)}) collective-permute-start(bf16[2,64,2560]{2,1,0:T(8,128)(2,1)S(1)} %bitcast.193), channel_id=1, source_target_pairs={{0,8},{8,0},{16,24},{24,16},{1,9},{9,1},{17,25},{25,17},{2,10},{10... | collective-permute-start | bytes 1966088 | tf_op jit(solution)/shard_map/ppermute | solution.py:28
  316.0 14.6 %collective-permute-start.37 = (bf16[32,4096]{1,0:T(8,128)(2,1)}, bf16[32,4096]{1,0:T(8,128)(2,1)S(1)}, u32[]{:S(2)}, u32[]{:S(2)}) collective-permute-start(bf16[32,4096]{1,0:T(8,128)(2,1)} %get-tuple-element.27), channel_id=1, source_target_pairs={{0,4},{4,0},{8,12},{12,8},{16,20},{20,16},{24,28},{28,24},{1,5},{5... | collective-permute-start | bytes 786440 | tf_op jit(solution)/shard_map/ppermute | solution.py:72
  317.5 13.1 %collective-permute-start.38 = (bf16[32,4096]{1,0:T(8,128)(2,1)}, bf16[32,4096]{1,0:T(8,128)(2,1)S(1)}, u32[]{:S(2)}, u32[]{:S(2)}) collective-permute-start(bf16[32,4096]{1,0:T(8,128)(2,1)} %get-tuple-element.27), channel_id=1, source_target_pairs={{0,20},{4,16},{8,28},{12,24},{16,4},{20,0},{24,12},{28,8},{1,21},{... | collective-permute-start | bytes 786440 | tf_op jit(solution)/shard_map/ppermute | solution.py:72
  (25 other events, 198.8 us)
Sparse Core Ops, SparseCore 0:
  181.3 38.4 all-gather.2
  221.4 38.0 all-gather.4
  316.1 62.5 reduce-scatter.1

commit v2 on v1

--- a/solution.py
+++ b/solution.py
@@ -49,6 +49,17 @@
     out = value[None]
     for step in bits(lax.axis_size(axis))[::-1]:
         out = join(out, axis, step, 0)
+    return out
+
+
+def direct(value, axis):
+    n = lax.axis_size(axis)
+    index = lax.axis_index(axis)
+    out = jnp.zeros((n,) + value.shape, value.dtype)
+    out = lax.dynamic_update_slice_in_dim(out, value[None], index, 0)
+    for step in range(1, n):
+        got = swap(value, axis, step)[None]
+        out = lax.dynamic_update_slice_in_dim(out, got, index ^ step, 0)
     return out
 
 
@@ -119,18 +130,19 @@
     return [(n - 1 - i, n - 1 - j) for i, j in right_of(n, tick, gather)]
 
 
-def line_scatter(parts, axis):
+def line_scatter(part, lo, span, rows, axis):
     n = lax.axis_size(axis)
     z = lax.axis_index(axis)
 
-    def block(s):
-        s = jnp.clip(s, 0, n - 1)
-        blocks = [lax.dynamic_index_in_dim(p, s, 0, keepdims=False) for p in parts]
+    def block(source, s):
+        at = jnp.clip(s, 0, n - 1) * rows
+        blocks = [lax.dynamic_slice(source, (k, at, lo), (1, rows, span))[0] for k in range(2)]
         return jnp.concatenate(blocks, axis=-1)
 
     right = left = None
     for tick in range(1, n):
-        to_right, to_left = block(n + z - tick), block(z + tick - n)
+        source = part if tick == 1 else tied(part, right)
+        to_right, to_left = block(source, n + z - tick), block(source, z + tick - n)
         if tick > 1:
             to_right, to_left = to_right + right, to_left + left
         right = (to_right * gate_scale).astype(f16)
@@ -138,7 +150,7 @@
         right = lax.ppermute(right, axis, right_of(n, tick, False))
         left = lax.ppermute(left, axis, left_of(n, tick, False))
         right, left = (v.astype(f32) * (1.0 / gate_scale) for v in (right, left))
-    return block(z) + right + left
+    return block(tied(part, right), z) + right + left
 
 
 def back_kernel(grads_ref, gate_ref, up_ref, *refs):
@@ -183,7 +195,7 @@
         out_specs=out_spec,
         out_shape=jax.ShapeDtypeStruct((rows, width), f32),
         input_output_aliases={3: 0} if so_far is not None else {},
-        compiler_params=pltpu.CompilerParams(vmem_limit_bytes=48 * 2**20),
+        compiler_params=pltpu.CompilerParams(vmem_limit_bytes=60 * 1024 * 2**10),
         cost_estimate=pl.CostEstimate(
             flops=4 * rows * span * width,
             bytes_accessed=4 * width * span + 4 * rows * span + 4 * rows * width,
@@ -211,49 +223,54 @@
     is_text = (places < audio_len[0] + text_len[0])[:, None]
     text_rows = jnp.where(is_text, text_embed.astype(f32), 0.0)
 
-    def inverse(squares):
-        total = line_sum(squares, "width")
-        return lax.rsqrt(total / full_width + norm_eps)[:, None]
-
-    tail = text_rows[cap:]
-    tail_squares = jnp.sum(tail * tail, axis=1)
-    tail_norm = (tail * inverse(tail_squares) * gain).astype(bf16)
-    tail_rows = spread(tail_norm, "batch")
+    tail_all = spread(jnp.where(is_text[cap:], text_embed[cap:], 0), "batch")
 
     stacked = frames[0, : 4 * cap].reshape(cap, 4 * feat_here)
     kernel = adapter_weight.reshape(4 * feat_here, width_here)
     half = width_here // 2
     pieces = []
     for lo in (0, half):
-        audio = jnp.dot(tied(stacked, tail_squares), kernel[:, lo : lo + half], preferred_element_type=f32)
         for step in bits(lax.axis_size("hidden")):
-            got = swap((audio * audio_scale).astype(f16), "hidden", step)
+            if step == 1:
+                audio = jnp.dot(
+                    stacked, kernel[:, lo : lo + half], preferred_element_type=f32
+                )
+            sent = (audio * audio_scale).astype(f16)
+            got = swap(sent, "hidden", step)
             audio = audio + got.astype(f32) * (1.0 / audio_scale)
         pieces.append(audio)
     audio = jnp.concatenate(pieces, axis=1)
     head = jnp.where(is_audio, audio, text_rows[:cap])
-    inv_rms = inverse(jnp.sum(head * head, axis=1))
-    unit = head * inv_rms
-    head_rows = spread((unit * gain).astype(bf16), "batch")
-    count = head_rows.shape[0]
+    head_all = spread((head * audio_scale).astype(f16), "batch")
+    count = head_all.shape[0]
     n_head = count * cap
-
-    rows = jnp.concatenate([head_rows, tail_rows], axis=0).reshape(2 * n_head, width_here)
+    tail = text_rows[cap:]
+    squares = jnp.concatenate([jnp.sum(head * head, axis=1), jnp.sum(tail * tail, axis=1)])
+    inv_own = lax.rsqrt(line_sum(squares, "width") / full_width + norm_eps)
+    inv_all = direct(inv_own, "batch")
+    inv_rms = inv_own[:, None]
+    unit = head * inv_rms[:cap]
+    rows = jnp.stack([head_all.astype(f32) * (1.0 / audio_scale), tail_all.astype(f32)])
+    scales = jnp.stack([inv_all[:, :cap], inv_all[:, cap:]])[..., None]
+    rows = (rows * scales * gain).astype(bf16).reshape(2 * n_head, width_here)
     part = jnp.einsum("tf,fgh->gth", rows, gate_up, preferred_element_type=f32)
     part = lax.optimization_barrier(part)
     stack_all = spread(tied(stacked, part), "batch").reshape(n_head, 4 * feat_here)
-
-    def chunk(c):
-        return [part[k, :n_head, c * span : (c + 1) * span] for k in range(2)]
 
     def gates(summed):
         gate, up = jnp.split(summed, 2, axis=1)
         sig = jax.nn.sigmoid(gate)
         return gate, up, sig, gate * sig
 
+    rest = lax.optimization_barrier((part[0, n_head:], part[1, n_head:]))
+    rest = jnp.concatenate([p.astype(bf16) for p in rest], axis=1)
     hidden_head, pairs, proj = [], [], 0.0
     for c in range(chunks):
-        got = line_scatter([p.reshape(count, cap, span) for p in chunk(c)], "width")
+        got = line_scatter(part, c * span, span, cap, "width")
+        if c == 0:
+            got, stack_all, rest = lax.optimization_barrier((got, stack_all, rest))
+        if c:
+            got = tied(got, grads)
         gate, up, sig, silu = gates(got)
         hidden_head.append((silu * up).astype(bf16))
         cot = cotangent[:cap, c * span : (c + 1) * span].astype(f32)
@@ -265,8 +282,6 @@
 
     last = pairs[-1]
     w = lax.optimization_barrier(tied(gate_up, grads).reshape(width_here, 2 * units))
-    rest = lax.optimization_barrier((part[0, n_head:], part[1, n_head:], grads))[:2]
-    rest = jnp.concatenate([p.astype(bf16) for p in rest], axis=1)
     proj = tied(proj, grads)
 
     lines = lax.axis_size("width")
@@ -281,7 +296,7 @@
         for step in bits(lax.axis_size(axis)):
             shared = shared + swap(shared, axis, step)
 
-    pairs[-1], shared, rest = lax.optimization_barrier((pairs[-1], shared, rest))
+    pairs[0], shared = lax.optimization_barrier((pairs[0], shared))
     grad = None
     for c in range(chunks):
         grad = back(pairs[c], w, c, chunks, grad)

time: 388 us -> 386 us (level)
  waiting for transfers between devices: 141 us -> 107 us
  other arithmetic: 18 us -> 36.8 us
  Pallas kernels: 28.6 us -> 33.5 us
  starting transfers between devices: 57 us -> 61.3 us
  local copies, waits for them, and re-layouts: 53.3 us -> 57.3 us
    all_gather x2, waiting for transfers between devices: 24.6 us -> 0.02 us  [on_device(): pairs.append(lax.all_gather(grads, 'width', axis=0, tiled=True))]
    ppermute x6, waiting for transfers between devices: 29.1 us -> 10.1 us  [line_scatter(): right = lax.ppermute(right, axis, right_of(n, tick, False))]
    ppermute x6, waiting for transfers between devices: 0.02 us -> 16.3 us  [line_scatter(): left = lax.ppermute(left, axis, left_of(n, tick, False))]
    ppermute x13 -> x16, waiting for transfers between devices: 31.4 us -> 22.6 us  [swap(): lax.ppermute(value, axis, [(i, i ^ step) for i in range(lax.axis_size(axi...]
    squeeze x3, local copies, waits for them, and re-layouts: 4.27 us -> 10.1 us  [the longest x2 6.74 us: block(): lax.dynamic_slice(source, (k, at, lo), (1, rows, span))[0]]
    pallas_call x2, Pallas kernels: 28.6 us -> 33.5 us  [back(): pl.pallas_call(back_kernel, grid=(width // block,), in_specs=in_specs, ou...]
    ppermute x6 -> x3, starting transfers between devices: 10.4 us -> 5.52 us  [line_sum(): lax.ppermute(value, axis, [(i, (i + shift) % n) for i in range(n)])]
    convert_element_type x6, other arithmetic: 0.8 us -> 5.34 us  [line_scatter(): left = (to_left * gate_scale).astype(f16)]
  transfers between devices with their start and end apart: 43 -> 43, of which waited for: 24 -> 21; matrix products, arithmetic and copies ran while one was open for 22% -> 26% of each run, Pallas kernels for 0% -> 4%
where the time goes in v2:
time: 386 us; the launch traced here: 385 us
  waiting for transfers between devices  107 us (28%)
  matrix products  73.7 us (19%)
  starting transfers between devices  61.3 us (16%)
  local copies, waits for them, and re-layouts  57.3 us (15%)
  other arithmetic  36.8 us (10%)
  Pallas kernels  33.5 us (9%)
  between operations  15.9 us (4%)
    dot_general x1, matrix products, on_device(): part = jnp.einsum('tf,fgh->gth', rows, gate_up, preferred_element_type=f32)  42.7 us
    unnamed x27, local copies, waits for them, and re-layouts  37.7 us
    pallas_call x2, Pallas kernels, back(): pl.pallas_call(back_kernel, grid=(width // block,), in_specs=in_specs, ou...  33.5 us
    reduce_scatter x1, waiting for transfers between devices, on_device(): lax.psum_scatter(tied(rest, last), 'width', scatter_dimension=0, tiled=True)  31.5 us
    ppermute x6, waiting for transfers between devices, quad_swap(): return lax.ppermute(value, axes, pairs)  22.7 us
    ppermute x16, waiting for transfers between devices, swap(): lax.ppermute(value, axis, [(i, i ^ step) for i in range(lax.axis_size(axi...  22.6 us
    ppermute x6, starting transfers between devices, line_scatter(): right = lax.ppermute(right, axis, right_of(n, tick, False))  20.4 us
    dot_general x1, matrix products, on_device(): lax.dot_general(stack_all, grad.reshape(n_head, width_here), (((0,), (0,)...  17.4 us
  transfers between devices with their start and end apart: 43, of which 21 were waited for; matrix products, arithmetic and copies ran while one was open for 26% of the time, Pallas kernels for 4%

profile of v2, /device:TPU:0, one launch (start us, length us, event | category | flops | bytes accessed | tf_op | source)
XLA Modules:
  0.0 385.2 jit_solution(1385236694519139712)
XLA Ops:
  8.4 6.8 %multiply_convert_fusion.1 = (f16[64,2048]{1,0:T(8,128)(2,1)}, f32[64,2048]{1,0:T(8,128)}) fusion(bf16[64,2560]{1,0:T(8,128)(2,1)S(1)} %reshape_squeeze.3, bf16[2560,4096]{1,0:T(8,128)(2,1)} %bitcast.206), kind=kOutput, calls=%fused_computation.102 | convolution fusion | flops 671350784 | bytes 11599872 | tf_op jit(solution)/shard_map/dot_general | solution.py:235
  15.2 3.0 collective-permute-start.1
  18.2 6.8 %multiply_convert_fusion.2 = (f16[64,2048]{1,0:T(8,128)(2,1)}, f32[64,2048]{1,0:T(8,128)}) fusion(bf16[64,2560]{1,0:T(8,128)(2,1)S(1)} %reshape_squeeze.3, bf16[2560,4096]{1,0:T(8,128)(2,1)} %bitcast.207), kind=kOutput, calls=%fused_computation.104 | convolution fusion | flops 671350784 | bytes 11599872 | tf_op jit(solution)/shard_map/dot_general | solution.py:235
  36.3 2.6 collective-permute-start.7
  46.2 11.5 %collective-permute-done.11 = f32[128]{0:T(128)S(1)} collective-permute-done((f32[128]{0:T(128)S(1)}, f32[128]{0:T(128)S(1)}, u32[]{:S(2)}, u32[]{:S(2)}) %collective-permute-start.11) | collective-permute-done | bytes 544 | tf_op jit(solution)/shard_map/ppermute | solution.py:28
  67.2 3.6 fusion.10
  70.8 42.7 %fusion.6 = f32[2,512,3328]{2,1,0:T(8,128)} fusion(bf16[4096,2,3328]{2,1,0:T(2,128)(2,1)} %param.14, bf16[512,4096]{1,0:T(8,128)(2,1)} %fusion.10), kind=kOutput, calls=%fused_computation.6 | convolution fusion | flops 27917287424 | bytes 72351744 | tf_op jit(solution)/shard_map/tf,fgh->gth/dot_general | solution.py:256
  113.5 3.3 slice_bitcast_fusion
  120.5 2.9 collective-permute-start.12
  132.1 4.6 %dynamic-slice_bitcast_fusion.11 = (f32[64,1664]{1,0:T(8,128)S(1)}, f32[64,1664]{1,0:T(8,128)S(1)}, f32[64,1664]{1,0:T(8,128)S(1)}, f32[64,1664]{1,0:T(8,128)S(1...) fusion(f32[2,512,3328]{2,1,0:T(8,128)} %fusion.6, ...), kind=kLoop, calls=%fused_computation.129 | loop fusion | bytes 17039380 | tf_op jit(solution)/shard_map/squeeze | solution.py:139
  143.2 4.4 %collective-permute-start.21 = (f16[64,3328]{1,0:T(8,128)(2,1)S(1)}, f16[64,3328]{1,0:T(8,128)(2,1)S(1)}, u32[]{:S(2)}, u32[]{:S(2)}) collective-permute-start(f16[64,3328]{1,0:T(8,128)(2,1)S(1)} %fusion.28), channel_id=1, source_target_pairs={{0,1},{1,2},{4,5},{5,6},{8,9},{9,10},{12,13},{13,14},{16,17},{17,1... | collective-permute-start | bytes 1277960 | tf_op jit(solution)/shard_map/ppermute | solution.py:150
  151.2 4.6 %collective-permute-start.14 = (f16[64,3328]{1,0:T(8,128)(2,1)S(1)}, f16[64,3328]{1,0:T(8,128)(2,1)S(1)}, u32[]{:S(2)}, u32[]{:S(2)}) collective-permute-start(f16[64,3328]{1,0:T(8,128)(2,1)S(1)} %fusion.19), channel_id=1, source_target_pairs={{0,1},{1,2},{2,3},{4,5},{5,6},{6,7},{8,9},{9,10},{10,11},{12,13},{... | collective-permute-start | bytes 1277960 | tf_op jit(solution)/shard_map/ppermute | solution.py:150
  157.3 2.9 collective-permute-done.21
  161.0 5.1 %collective-permute-start.22 = (f16[64,3328]{1,0:T(8,128)(2,1)}, f16[64,3328]{1,0:T(8,128)(2,1)}, u32[]{:S(2)}, u32[]{:S(2)}) collective-permute-start(f16[64,3328]{1,0:T(8,128)(2,1)} %fusion.30), channel_id=1, source_target_pairs={{0,1},{1,2},{2,3},{4,5},{5,6},{6,7},{8,9},{9,10},{10,11},{12,13},{... | collective-permute-start | bytes 1277960 | tf_op jit(solution)/shard_map/ppermute | solution.py:150
  166.3 3.0 collective-permute-done.14
  174.1 3.6 collective-permute-done.22
  177.7 16.2 %collective-permute-done.25 = f16[64,3328]{1,0:T(8,128)(2,1)S(1)} collective-permute-done((f16[64,3328]{1,0:T(8,128)(2,1)S(1)}, f16[64,3328]{1,0:T(8,128)(2,1)S(1)}, u32[]{:S(2)}, u32[]{:S(2)}) %collective-permute-start.25) | collective-permute-done | bytes 426016 | tf_op jit(solution)/shard_map/ppermute | solution.py:151
  198.1 5.8 %collective-permute-start.26 = (f32[64]{0:T(128)S(1)}, f32[64]{0:T(128)S(1)}, u32[]{:S(2)}, u32[]{:S(2)}) collective-permute-start(f32[64]{0:T(128)S(1)} %add.367), channel_id=1, source_target_pairs={{0,1},{1,2},{2,3},{3,0},{4,5},{5,6},{6,7},{7,4},{8,9},{9,10},{10,1... | collective-permute-start | bytes 776 | tf_op jit(solution)/shard_map/ppermute | solution.py:293
  204.0 2.4 collective-permute-start.28
  206.5 2.2 collective-permute-done.27
  213.5 36.7 %copy.22 = bf16[512,8,2,3328]{3,1,2,0:T(8,128)(2,1)} copy(bf16[512,8,2,3328]{3,2,1,0:T(2,128)(2,1)} %bitcast.185) | data formatting | bytes 109051904
  250.3 16.2 %shard_map.95.refs_0_ = f32[256,4096]{1,0:T(8,128)} custom-call(bf16[256,3328]{1,0:T(8,128)(2,1)} %all-gather.5.cloned.1.call-done.grads_ref, bf16[4096,6656]{1,0:T(8,128)(2,1)} %bitcast.181, bf16[4096,6656]{1,0:T(8,128)(2,1)} %bitcast.182), custom_call_target="tpu_custom_call" | custom-call | flops 6979321856 | bytes 33161216 | tf_op jit(solution)/shard_map/pallas_call | solution.py:191
  266.5 17.3 %shard_map.96 = f32[256,4096]{1,0:T(8,128)} custom-call(bf16[256,3328]{1,0:T(8,128)(2,1)} %all-gather.3.cloned.1.call-done.grads_ref, bf16[4096,6656]{1,0:T(8,128)(2,1)} %bitcast.183, bf16[4096,6656]{1,0:T(8,128)(2,1)} %bitcast.184, f32[256,4096]{1,0:T(8,128)} %shard_map.95.refs_0_), custom_call_target="tpu_custom_call", output_to_operand_aliasing={{}: (3, {})} | custom-call | flops 6979321856 | bytes 33161216 | tf_op jit(solution)/shard_map/pallas_call | solution.py:191
  285.8 2.5 collective-permute-done.32
  291.0 2.3 collective-permute-start.33
  295.0 5.8 %collective-permute-done.33 = bf16[32,4096]{1,0:T(8,128)(2,1)} collective-permute-done((bf16[32,4096]{1,0:T(8,128)(2,1)}, bf16[32,4096]{1,0:T(8,128)(2,1)}, u32[]{:S(2)}, u32[]{:S(2)}) %collective-permute-start.33) | collective-permute-done | bytes 262176 | tf_op jit(solution)/shard_map/ppermute | solution.py:83
  300.7 6.5 %collective-permute-done.34 = bf16[32,4096]{1,0:T(8,128)(2,1)} collective-permute-done((bf16[32,4096]{1,0:T(8,128)(2,1)}, bf16[32,4096]{1,0:T(8,128)(2,1)}, u32[]{:S(2)}, u32[]{:S(2)}) %collective-permute-start.34) | collective-permute-done | bytes 262176 | tf_op jit(solution)/shard_map/ppermute | solution.py:83
  314.0 5.8 %collective-permute-done.36 = bf16[32,4096]{1,0:T(8,128)(2,1)S(1)} collective-permute-done((bf16[32,4096]{1,0:T(8,128)(2,1)}, bf16[32,4096]{1,0:T(8,128)(2,1)S(1)}, u32[]{:S(2)}, u32[]{:S(2)}) %collective-permute-start.36) | collective-permute-done | bytes 262176 | tf_op jit(solution)/shard_map/ppermute | solution.py:83
  319.8 4.6 %collective-permute-done.37 = bf16[32,4096]{1,0:T(8,128)(2,1)S(1)} collective-permute-done((bf16[32,4096]{1,0:T(8,128)(2,1)}, bf16[32,4096]{1,0:T(8,128)(2,1)S(1)}, u32[]{:S(2)}, u32[]{:S(2)}) %collective-permute-start.37) | collective-permute-done | bytes 262176 | tf_op jit(solution)/shard_map/ppermute | solution.py:83
  324.9 2.3 collective-permute-done.39
  327.4 17.4 %fusion.63 = f32[2560,4096]{1,0:T(8,128)} fusion(bf16[256,2560]{1,0:T(8,128)(2,1)S(1)} %bitcast.192, bf16[256,4096]{1,0:T(8,128)(2,1)S(1)} %bitcast.191), kind=kOutput, calls=%fused_computation.169 | convolution fusion | flops 5368709120 | bytes 45350912 | tf_op jit(solution)/shard_map/dot_general | solution.py:323
  344.7 31.5 %reduce-scatter.2.cloned.1.call-done = bf16[64,6656]{1,0:T(8,128)(2,1)} async-done(((bf16[256,6656]{1,0:T(8,128)(2,1)}), bf16[64,6656]{1,0:T(8,128)(2,1)}) %reduce-scatter.2.cloned.1.call-update) | async-done | bytes 851984 | tf_op jit(solution)/shard_map/reduce_scatter | solution.py:330
  (186 shorter events, 82.4 us)
Async XLA Ops:
  7.2 243.1 %all-gather.5.cloned.1.call-start = ((), (), s32[]{:S(2)}) async-start(), calls=%async_computation.3 | async-start | bytes 2129920 | tf_op jit(solution)/shard_map/all_gather | solution.py:281
  15.2 15.9 %collective-permute-start.1 = (f16[64,2048]{1,0:T(8,128)(2,1)}, f16[64,2048]{1,0:T(8,128)(2,1)}, u32[]{:S(2)}, u32[]{:S(2)}) collective-permute-start(f16[64,2048]{1,0:T(8,128)(2,1)} %get-tuple-element.90), channel_id=1, source_target_pairs={{0,4},{4,0},{1,5},{5,1},{2,6},{6,2},{3,7},{7,3},{8,12},{12,8},{9,1... | collective-permute-start | bytes 786440 | tf_op jit(solution)/shard_map/ppermute | solution.py:28
  25.1 8.1 %collective-permute-start = (f16[64,2048]{1,0:T(8,128)(2,1)}, f16[64,2048]{1,0:T(8,128)(2,1)}, u32[]{:S(2)}, u32[]{:S(2)}) collective-permute-start(f16[64,2048]{1,0:T(8,128)(2,1)} %get-tuple-element.92), channel_id=1, source_target_pairs={{0,4},{4,0},{1,5},{5,1},{2,6},{6,2},{3,7},{7,3},{8,12},{12,8},{9,1... | collective-permute-start | bytes 786440 | tf_op jit(solution)/shard_map/ppermute | solution.py:28
  27.5 30.5 %collective-permute-start.4 = (bf16[1,64,4096]{2,1,0:T(8,128)(2,1)}, bf16[1,64,4096]{2,1,0:T(8,128)(2,1)}, u32[]{:S(2)}, u32[]{:S(2)}) collective-permute-start(bf16[1,64,4096]{2,1,0:T(8,128)(2,1)} %fusion.57), channel_id=1, source_target_pairs={{0,16},{8,24},{16,0},{24,8},{1,17},{9,25},{17,1},{25,9},{2,18},{10... | collective-permute-start | bytes 1572872 | tf_op jit(solution)/shard_map/ppermute | solution.py:28
  34.7 6.4 %collective-permute-start.6 = (f32[128]{0:T(128)S(1)}, f32[128]{0:T(128)S(1)}, u32[]{:S(2)}, u32[]{:S(2)}) collective-permute-start(f32[128]{0:T(128)S(1)} %pad_maximum_fusion.6), channel_id=1, source_target_pairs={{0,1},{1,2},{2,3},{3,0},{4,5},{5,6},{6,7},{7,4},{8,9},{9,10},{10,1... | collective-permute-start | bytes 1544 | tf_op jit(solution)/shard_map/ppermute | solution.py:121
  36.3 4.8 %collective-permute-start.7 = (f32[128]{0:T(128)S(1)}, f32[128]{0:T(128)S(1)}, u32[]{:S(2)}, u32[]{:S(2)}) collective-permute-start(f32[128]{0:T(128)S(1)} %pad_maximum_fusion.6), channel_id=1, source_target_pairs={{0,2},{1,3},{2,0},{3,1},{4,6},{5,7},{6,4},{7,5},{8,10},{9,11},{10,... | collective-permute-start | bytes 1544 | tf_op jit(solution)/shard_map/ppermute | solution.py:121
  44.3 16.4 %collective-permute-start.2 = (f16[1,64,4096]{2,1,0:T(8,128)(2,1)}, f16[1,64,4096]{2,1,0:T(8,128)(2,1)}, u32[]{:S(2)}, u32[]{:S(2)}) collective-permute-start(f16[1,64,4096]{2,1,0:T(8,128)(2,1)} %fusion.56), channel_id=1, source_target_pairs={{0,16},{8,24},{16,0},{24,8},{1,17},{9,25},{17,1},{25,9},{2,18},{10... | collective-permute-start | bytes 1572872 | tf_op jit(solution)/shard_map/ppermute | solution.py:28
  44.9 12.8 %collective-permute-start.11 = (f32[128]{0:T(128)S(1)}, f32[128]{0:T(128)S(1)}, u32[]{:S(2)}, u32[]{:S(2)}) collective-permute-start(f32[128]{0:T(128)S(1)} %add_rsqrt_fusion), channel_id=1, source_target_pairs={{0,24},{8,16},{16,8},{24,0},{1,25},{9,17},{17,9},{25,1},{2,26},{10... | collective-permute-start | bytes 1544 | tf_op jit(solution)/shard_map/ppermute | solution.py:28
  116.9 19.7 %collective-permute-start.18 = (bf16[1,64,2560]{2,1,0:T(8,128)(2,1)S(1)}, bf16[1,64,2560]{2,1,0:T(8,128)(2,1)S(1)}, u32[]{:S(2)}, u32[]{:S(2)}) collective-permute-start(bf16[1,64,2560]{2,1,0:T(8,128)(2,1)S(1)} %bitcast.196), channel_id=1, source_target_pairs={{0,16},{8,24},{16,0},{24,8},{1,17},{9,25},{17,1},{25,9},{2,18},{10... | collective-permute-start | bytes 983048 | tf_op jit(solution)/shard_map/ppermute | solution.py:28
  120.5 16.4 %collective-permute-start.12 = (f16[64,3328]{1,0:T(8,128)(2,1)}, f16[64,3328]{1,0:T(8,128)(2,1)}, u32[]{:S(2)}, u32[]{:S(2)}) collective-permute-start(f16[64,3328]{1,0:T(8,128)(2,1)} %fusion.15), channel_id=1, source_target_pairs={{0,1},{4,5},{8,9},{12,13},{16,17},{20,21},{24,25},{28,29}} | collective-permute-start | bytes 1277960 | tf_op jit(solution)/shard_map/ppermute | solution.py:150
  124.3 15.2 %collective-permute-start.15 = (f16[64,3328]{1,0:T(8,128)(2,1)}, f16[64,3328]{1,0:T(8,128)(2,1)}, u32[]{:S(2)}, u32[]{:S(2)}) collective-permute-start(f16[64,3328]{1,0:T(8,128)(2,1)} %fusion.25), channel_id=1, source_target_pairs={{3,2},{7,6},{11,10},{15,14},{19,18},{23,22},{27,26},{31,30}} | collective-permute-start | bytes 1277960 | tf_op jit(solution)/shard_map/ppermute | solution.py:151
  126.5 15.5 %collective-permute-start.20 = (f16[64,3328]{1,0:T(8,128)(2,1)}, f16[64,3328]{1,0:T(8,128)(2,1)}, u32[]{:S(2)}, u32[]{:S(2)}) collective-permute-start(f16[64,3328]{1,0:T(8,128)(2,1)} %fusion.26), channel_id=1, source_target_pairs={{0,1},{4,5},{8,9},{12,13},{16,17},{20,21},{24,25},{28,29}} | collective-permute-start | bytes 1277960 | tf_op jit(solution)/shard_map/ppermute | solution.py:150
  128.7 18.9 %collective-permute-start.23 = (f16[64,3328]{1,0:T(8,128)(2,1)S(1)}, f16[64,3328]{1,0:T(8,128)(2,1)}, u32[]{:S(2)}, u32[]{:S(2)}) collective-permute-start(f16[64,3328]{1,0:T(8,128)(2,1)S(1)} %fusion.36), channel_id=1, source_target_pairs={{3,2},{7,6},{11,10},{15,14},{19,18},{23,22},{27,26},{31,30}} | collective-permute-start | bytes 1277960 | tf_op jit(solution)/shard_map/ppermute | solution.py:151
  136.7 29.5 %collective-permute-start.19 = (bf16[2,64,2560]{2,1,0:T(8,128)(2,1)S(1)}, bf16[2,64,2560]{2,1,0:T(8,128)(2,1)S(1)}, u32[]{:S(2)}, u32[]{:S(2)}) collective-permute-start(bf16[2,64,2560]{2,1,0:T(8,128)(2,1)S(1)} %bitcast.195), channel_id=1, source_target_pairs={{0,8},{8,0},{16,24},{24,16},{1,9},{9,1},{17,25},{25,17},{2,10},{10... | collective-permute-start | bytes 1966088 | tf_op jit(solution)/shard_map/ppermute | solution.py:28
  138.1 12.9 %collective-permute-start.13 = (f16[64,3328]{1,0:T(8,128)(2,1)S(1)}, f16[64,3328]{1,0:T(8,128)(2,1)S(1)}, u32[]{:S(2)}, u32[]{:S(2)}) collective-permute-start(f16[64,3328]{1,0:T(8,128)(2,1)S(1)} %fusion.17), channel_id=1, source_target_pairs={{0,1},{1,2},{4,5},{5,6},{8,9},{9,10},{12,13},{13,14},{16,17},{17,1... | collective-permute-start | bytes 1277960 | tf_op jit(solution)/shard_map/ppermute | solution.py:150
  140.6 15.2 %collective-permute-start.16 = (f16[64,3328]{1,0:T(8,128)(2,1)S(1)}, f16[64,3328]{1,0:T(8,128)(2,1)S(1)}, u32[]{:S(2)}, u32[]{:S(2)}) collective-permute-start(f16[64,3328]{1,0:T(8,128)(2,1)S(1)} %fusion.24), channel_id=1, source_target_pairs={{3,2},{2,1},{7,6},{6,5},{11,10},{10,9},{15,14},{14,13},{19,18},{18... | collective-permute-start | bytes 1277960 | tf_op jit(solution)/shard_map/ppermute | solution.py:151
  143.2 17.0 %collective-permute-start.21 = (f16[64,3328]{1,0:T(8,128)(2,1)S(1)}, f16[64,3328]{1,0:T(8,128)(2,1)S(1)}, u32[]{:S(2)}, u32[]{:S(2)}) collective-permute-start(f16[64,3328]{1,0:T(8,128)(2,1)S(1)} %fusion.28), channel_id=1, source_target_pairs={{0,1},{1,2},{4,5},{5,6},{8,9},{9,10},{12,13},{13,14},{16,17},{17,1... | collective-permute-start | bytes 1277960 | tf_op jit(solution)/shard_map/ppermute | solution.py:150
  149.5 22.1 %collective-permute-start.24 = (f16[64,3328]{1,0:T(8,128)(2,1)}, f16[64,3328]{1,0:T(8,128)(2,1)}, u32[]{:S(2)}, u32[]{:S(2)}) collective-permute-start(f16[64,3328]{1,0:T(8,128)(2,1)} %fusion.35), channel_id=1, source_target_pairs={{3,2},{2,1},{7,6},{6,5},{11,10},{10,9},{15,14},{14,13},{19,18},{18... | collective-permute-start | bytes 1277960 | tf_op jit(solution)/shard_map/ppermute | solution.py:151
  151.2 18.1 %collective-permute-start.14 = (f16[64,3328]{1,0:T(8,128)(2,1)S(1)}, f16[64,3328]{1,0:T(8,128)(2,1)S(1)}, u32[]{:S(2)}, u32[]{:S(2)}) collective-permute-start(f16[64,3328]{1,0:T(8,128)(2,1)S(1)} %fusion.19), channel_id=1, source_target_pairs={{0,1},{1,2},{2,3},{4,5},{5,6},{6,7},{8,9},{9,10},{10,11},{12,13},{... | collective-permute-start | bytes 1277960 | tf_op jit(solution)/shard_map/ppermute | solution.py:150
  156.0 13.3 %collective-permute-start.17 = (f16[64,3328]{1,0:T(8,128)(2,1)S(1)}, f16[64,3328]{1,0:T(8,128)(2,1)S(1)}, u32[]{:S(2)}, u32[]{:S(2)}) collective-permute-start(f16[64,3328]{1,0:T(8,128)(2,1)S(1)} %fusion.22), channel_id=1, source_target_pairs={{3,2},{2,1},{1,0},{7,6},{6,5},{5,4},{11,10},{10,9},{9,8},{15,14},{... | collective-permute-start | bytes 1277960 | tf_op jit(solution)/shard_map/ppermute | solution.py:151
  161.0 16.7 %collective-permute-start.22 = (f16[64,3328]{1,0:T(8,128)(2,1)}, f16[64,3328]{1,0:T(8,128)(2,1)}, u32[]{:S(2)}, u32[]{:S(2)}) collective-permute-start(f16[64,3328]{1,0:T(8,128)(2,1)} %fusion.30), channel_id=1, source_target_pairs={{0,1},{1,2},{2,3},{4,5},{5,6},{6,7},{8,9},{9,10},{10,11},{12,13},{... | collective-permute-start | bytes 1277960 | tf_op jit(solution)/shard_map/ppermute | solution.py:150
  171.6 94.9 %all-gather.3.cloned.1.call-start = ((), (), s32[]{:S(2)}) async-start(), calls=%async_computation.1 | async-start | bytes 2129920 | tf_op jit(solution)/shard_map/all_gather | solution.py:281
  172.8 21.1 %collective-permute-start.25 = (f16[64,3328]{1,0:T(8,128)(2,1)S(1)}, f16[64,3328]{1,0:T(8,128)(2,1)S(1)}, u32[]{:S(2)}, u32[]{:S(2)}) collective-permute-start(f16[64,3328]{1,0:T(8,128)(2,1)S(1)} %fusion.33), channel_id=1, source_target_pairs={{3,2},{2,1},{1,0},{7,6},{6,5},{5,4},{11,10},{10,9},{9,8},{15,14},{... | collective-permute-start | bytes 1277960 | tf_op jit(solution)/shard_map/ppermute | solution.py:151
  198.0 178.2 %reduce-scatter.2.cloned.1.call-start = ((), (), s32[]{:S(2)}) async-start(), calls=%async_computation.2 | async-start | bytes 4259840 | tf_op jit(solution)/shard_map/reduce_scatter | solution.py:330
  198.1 8.3 %collective-permute-start.26 = (f32[64]{0:T(128)S(1)}, f32[64]{0:T(128)S(1)}, u32[]{:S(2)}, u32[]{:S(2)}) collective-permute-start(f32[64]{0:T(128)S(1)} %add.367), channel_id=1, source_target_pairs={{0,1},{1,2},{2,3},{3,0},{4,5},{5,6},{6,7},{7,4},{8,9},{9,10},{10,1... | collective-permute-start | bytes 776 | tf_op jit(solution)/shard_map/ppermute | solution.py:293
  213.5 36.7 %collective-permute-start.31 = (f32[4,64]{1,0:T(4,128)S(1)}, f32[4,64]{1,0:T(4,128)S(1)}, u32[]{:S(2)}, u32[]{:S(2)}) collective-permute-start(f32[4,64]{1,0:T(4,128)S(1)} %add.376), channel_id=1, source_target_pairs={{0,4},{4,0},{1,5},{5,1},{2,6},{6,2},{3,7},{7,3},{8,12},{12,8},{9,1... | collective-permute-start | bytes 3080 | tf_op jit(solution)/shard_map/ppermute | solution.py:28
  291.0 9.8 %collective-permute-start.33 = (bf16[32,4096]{1,0:T(8,128)(2,1)}, bf16[32,4096]{1,0:T(8,128)(2,1)}, u32[]{:S(2)}, u32[]{:S(2)}) collective-permute-start(bf16[32,4096]{1,0:T(8,128)(2,1)} %get-tuple-element.82), channel_id=1, source_target_pairs={{0,16},{4,20},{8,24},{12,28},{16,0},{20,4},{24,8},{28,12},{1,17},{... | collective-permute-start | bytes 786440 | tf_op jit(solution)/shard_map/ppermute | solution.py:83
  293.3 14.0 %collective-permute-start.34 = (bf16[32,4096]{1,0:T(8,128)(2,1)}, bf16[32,4096]{1,0:T(8,128)(2,1)}, u32[]{:S(2)}, u32[]{:S(2)}) collective-permute-start(bf16[32,4096]{1,0:T(8,128)(2,1)} %get-tuple-element.84), channel_id=1, source_target_pairs={{0,4},{4,0},{8,12},{12,8},{16,20},{20,16},{24,28},{28,24},{1,5},{5... | collective-permute-start | bytes 786440 | tf_op jit(solution)/shard_map/ppermute | solution.py:83
  294.4 12.8 %collective-permute-start.35 = (bf16[32,4096]{1,0:T(8,128)(2,1)}, bf16[32,4096]{1,0:T(8,128)(2,1)}, u32[]{:S(2)}, u32[]{:S(2)}) collective-permute-start(bf16[32,4096]{1,0:T(8,128)(2,1)} %get-tuple-element.83), channel_id=1, source_target_pairs={{0,20},{4,16},{8,28},{12,24},{16,4},{20,0},{24,12},{28,8},{1,21},{... | collective-permute-start | bytes 786440 | tf_op jit(solution)/shard_map/ppermute | solution.py:83
  310.4 9.4 %collective-permute-start.36 = (bf16[32,4096]{1,0:T(8,128)(2,1)}, bf16[32,4096]{1,0:T(8,128)(2,1)S(1)}, u32[]{:S(2)}, u32[]{:S(2)}) collective-permute-start(bf16[32,4096]{1,0:T(8,128)(2,1)} %get-tuple-element.43), channel_id=1, source_target_pairs={{0,16},{4,20},{8,24},{12,28},{16,0},{20,4},{24,8},{28,12},{1,17},{... | collective-permute-start | bytes 786440 | tf_op jit(solution)/shard_map/ppermute | solution.py:83
  311.3 13.1 %collective-permute-start.37 = (bf16[32,4096]{1,0:T(8,128)(2,1)}, bf16[32,4096]{1,0:T(8,128)(2,1)S(1)}, u32[]{:S(2)}, u32[]{:S(2)}) collective-permute-start(bf16[32,4096]{1,0:T(8,128)(2,1)} %get-tuple-element.43), channel_id=1, source_target_pairs={{0,4},{4,0},{8,12},{12,8},{16,20},{20,16},{24,28},{28,24},{1,5},{5... | collective-permute-start | bytes 786440 | tf_op jit(solution)/shard_map/ppermute | solution.py:83
  312.3 12.2 %collective-permute-start.38 = (bf16[32,4096]{1,0:T(8,128)(2,1)}, bf16[32,4096]{1,0:T(8,128)(2,1)S(1)}, u32[]{:S(2)}, u32[]{:S(2)}) collective-permute-start(bf16[32,4096]{1,0:T(8,128)(2,1)} %get-tuple-element.43), channel_id=1, source_target_pairs={{0,20},{4,16},{8,28},{12,24},{16,4},{20,0},{24,12},{28,8},{1,21},{... | collective-permute-start | bytes 786440 | tf_op jit(solution)/shard_map/ppermute | solution.py:83
  (24 other events, 206.6 us)
Sparse Core Ops, SparseCore 0:
  171.7 44.0 all-gather.4
  217.9 39.1 all-gather.2
  311.4 64.7 reduce-scatter.1

commit v3 on v2

--- a/solution.py
+++ b/solution.py
@@ -262,13 +262,11 @@
         sig = jax.nn.sigmoid(gate)
         return gate, up, sig, gate * sig
 
-    rest = lax.optimization_barrier((part[0, n_head:], part[1, n_head:]))
-    rest = jnp.concatenate([p.astype(bf16) for p in rest], axis=1)
     hidden_head, pairs, proj = [], [], 0.0
     for c in range(chunks):
         got = line_scatter(part, c * span, span, cap, "width")
         if c == 0:
-            got, stack_all, rest = lax.optimization_barrier((got, stack_all, rest))
+            got, stack_all = lax.optimization_barrier((got, stack_all))
         if c:
             got = tied(got, grads)
         gate, up, sig, silu = gates(got)
@@ -283,6 +281,9 @@
     last = pairs[-1]
     w = lax.optimization_barrier(tied(gate_up, grads).reshape(width_here, 2 * units))
     proj = tied(proj, grads)
+    rest = tied(part, grads)
+    rest = lax.optimization_barrier((rest[0, n_head:], rest[1, n_head:]))
+    rest = jnp.concatenate([p.astype(bf16) for p in rest], axis=1)
 
     lines = lax.axis_size("width")
     z = lax.axis_index("width")
@@ -296,7 +297,7 @@
         for step in bits(lax.axis_size(axis)):
             shared = shared + swap(shared, axis, step)
 
-    pairs[0], shared = lax.optimization_barrier((pairs[0], shared))
+    pairs[0], shared, rest = lax.optimization_barrier((pairs[0], shared, rest))
     grad = None
     for c in range(chunks):
         grad = back(pairs[c], w, c, chunks, grad)

time: 386 us -> 391 us (1.013)
  waiting for transfers between devices: 107 us -> 117 us
  other arithmetic: 36.8 us -> 29.7 us
    ppermute x6, waiting for transfers between devices: 10.1 us -> 29.9 us  [line_scatter(): right = lax.ppermute(right, axis, right_of(n, tick, False))]
    ppermute x6, waiting for transfers between devices: 16.3 us -> 2.2 us  [line_scatter(): left = lax.ppermute(left, axis, left_of(n, tick, False))]
    ppermute x3, starting transfers between devices: 8.28 us -> 13 us  [on_device(): got = lax.ppermute(proj, 'width', ring)]
  transfers between devices with their start and end apart: 43 -> 43, of which waited for: 21 -> 23; matrix products, arithmetic and copies ran while one was open for 26% -> 25% of each run, Pallas kernels for 4% -> 4%
where the time goes in v3:
time: 391 us; the launch traced here: 390 us
  waiting for transfers between devices  117 us (30%)
  matrix products  73.7 us (19%)
  starting transfers between devices  62.3 us (16%)
  local copies, waits for them, and re-layouts  58.1 us (15%)
  Pallas kernels  33.5 us (9%)
  other arithmetic  29.7 us (8%)
  between operations  16 us (4%)
    dot_general x1, matrix products, on_device(): part = jnp.einsum('tf,fgh->gth', rows, gate_up, preferred_element_type=f32)  42.7 us
    unnamed x27, local copies, waits for them, and re-layouts  38.4 us
    pallas_call x2, Pallas kernels, back(): pl.pallas_call(back_kernel, grid=(width // block,), in_specs=in_specs, ou...  33.5 us
    reduce_scatter x1, waiting for transfers between devices, on_device(): lax.psum_scatter(tied(rest, last), 'width', scatter_dimension=0, tiled=True)  31.8 us
    ppermute x6, waiting for transfers between devices, line_scatter(): right = lax.ppermute(right, axis, right_of(n, tick, False))  29.9 us
    ppermute x16, waiting for transfers between devices, swap(): lax.ppermute(value, axis, [(i, i ^ step) for i in range(lax.axis_size(axi...  25.6 us
    ppermute x6, waiting for transfers between devices, quad_swap(): return lax.ppermute(value, axes, pairs)  22.5 us
    ppermute x6, starting transfers between devices, line_scatter(): right = lax.ppermute(right, axis, right_of(n, tick, False))  20.2 us
  transfers between devices with their start and end apart: 43, of which 23 were waited for; matrix products, arithmetic and copies ran while one was open for 25% of the time, Pallas kernels for 4%

profile of v3, /device:TPU:0, one launch (start us, length us, event | category | flops | bytes accessed | tf_op | source)
XLA Modules:
  0.0 390.0 jit_solution(9936133178652226922)
XLA Ops:
  10.5 3.0 collective-permute-start.4
  14.7 6.8 %multiply_convert_fusion.1 = (f16[64,2048]{1,0:T(8,128)(2,1)}, f32[64,2048]{1,0:T(8,128)}) fusion(bf16[64,2560]{1,0:T(8,128)(2,1)S(1)} %reshape_squeeze.3, bf16[2560,4096]{1,0:T(8,128)(2,1)} %bitcast.206), kind=kOutput, calls=%fused_computation.102 | convolution fusion | flops 671350784 | bytes 11599872 | tf_op jit(solution)/shard_map/dot_general | solution.py:235
  23.0 6.8 %multiply_convert_fusion.2 = (f16[64,2048]{1,0:T(8,128)(2,1)}, f32[64,2048]{1,0:T(8,128)}) fusion(bf16[64,2560]{1,0:T(8,128)(2,1)S(1)} %reshape_squeeze.3, bf16[2560,4096]{1,0:T(8,128)(2,1)} %bitcast.207), kind=kOutput, calls=%fused_computation.104 | convolution fusion | flops 671350784 | bytes 11599872 | tf_op jit(solution)/shard_map/dot_general | solution.py:235
  33.3 4.4 %collective-permute-done = f16[64,2048]{1,0:T(8,128)(2,1)} collective-permute-done((f16[64,2048]{1,0:T(8,128)(2,1)}, f16[64,2048]{1,0:T(8,128)(2,1)}, u32[]{:S(2)}, u32[]{:S(2)}) %collective-permute-start) | collective-permute-done | bytes 262176 | tf_op jit(solution)/shard_map/ppermute | solution.py:28
  39.3 3.6 collective-permute-start.8
  44.8 2.6 collective-permute-done.7
  52.0 10.6 %collective-permute-done.11 = f32[128]{0:T(128)S(1)} collective-permute-done((f32[128]{0:T(128)S(1)}, f32[128]{0:T(128)S(1)}, u32[]{:S(2)}, u32[]{:S(2)}) %collective-permute-start.11) | collective-permute-done | bytes 544 | tf_op jit(solution)/shard_map/ppermute | solution.py:28
  72.0 3.6 fusion.10
  75.6 42.7 %fusion.6 = f32[2,512,3328]{2,1,0:T(8,128)} fusion(bf16[4096,2,3328]{2,1,0:T(2,128)(2,1)} %param.14, bf16[512,4096]{1,0:T(8,128)(2,1)} %fusion.10), kind=kOutput, calls=%fused_computation.6 | convolution fusion | flops 27917287424 | bytes 72351744 | tf_op jit(solution)/shard_map/tf,fgh->gth/dot_general | solution.py:256
  126.5 4.6 %dynamic-slice_bitcast_fusion.11 = (f32[64,1664]{1,0:T(8,128)S(1)}, f32[64,1664]{1,0:T(8,128)S(1)}, f32[64,1664]{1,0:T(8,128)S(1)}, f32[64,1664]{1,0:T(8,128)S(1...) fusion(f32[2,512,3328]{2,1,0:T(8,128)} %fusion.6, ...), kind=kLoop, calls=%fused_computation.129 | loop fusion | bytes 17039380 | tf_op jit(solution)/shard_map/squeeze | solution.py:139
  133.9 3.5 collective-permute-start.13
  138.3 3.7 collective-permute-done.20
  142.1 5.2 %collective-permute-start.21 = (f16[64,3328]{1,0:T(8,128)(2,1)S(1)}, f16[64,3328]{1,0:T(8,128)(2,1)}, u32[]{:S(2)}, u32[]{:S(2)}) collective-permute-start(f16[64,3328]{1,0:T(8,128)(2,1)S(1)} %fusion.28), channel_id=1, source_target_pairs={{0,1},{1,2},{4,5},{5,6},{8,9},{9,10},{12,13},{13,14},{16,17},{17,1... | collective-permute-start | bytes 1277960 | tf_op jit(solution)/shard_map/ppermute | solution.py:150
  148.8 2.3 collective-permute-done.13
  151.3 4.4 %collective-permute-start.14 = (f16[64,3328]{1,0:T(8,128)(2,1)S(1)}, f16[64,3328]{1,0:T(8,128)(2,1)S(1)}, u32[]{:S(2)}, u32[]{:S(2)}) collective-permute-start(f16[64,3328]{1,0:T(8,128)(2,1)S(1)} %fusion.19), channel_id=1, source_target_pairs={{0,1},{1,2},{2,3},{4,5},{5,6},{6,7},{8,9},{9,10},{10,11},{12,13},{... | collective-permute-start | bytes 1277960 | tf_op jit(solution)/shard_map/ppermute | solution.py:150
  160.4 8.4 %collective-permute-done.14 = f16[64,3328]{1,0:T(8,128)(2,1)S(1)} collective-permute-done((f16[64,3328]{1,0:T(8,128)(2,1)S(1)}, f16[64,3328]{1,0:T(8,128)(2,1)S(1)}, u32[]{:S(2)}, u32[]{:S(2)}) %collective-permute-start.14) | collective-permute-done | bytes 426016 | tf_op jit(solution)/shard_map/ppermute | solution.py:150
  172.4 4.4 %collective-permute-start.22 = (f16[64,3328]{1,0:T(8,128)(2,1)S(1)}, f16[64,3328]{1,0:T(8,128)(2,1)S(1)}, u32[]{:S(2)}, u32[]{:S(2)}) collective-permute-start(f16[64,3328]{1,0:T(8,128)(2,1)S(1)} %fusion.30), channel_id=1, source_target_pairs={{0,1},{1,2},{2,3},{4,5},{5,6},{6,7},{8,9},{9,10},{10,11},{12,13},{... | collective-permute-start | bytes 1277960 | tf_op jit(solution)/shard_map/ppermute | solution.py:150
  176.9 15.5 %collective-permute-done.22 = f16[64,3328]{1,0:T(8,128)(2,1)S(1)} collective-permute-done((f16[64,3328]{1,0:T(8,128)(2,1)S(1)}, f16[64,3328]{1,0:T(8,128)(2,1)S(1)}, u32[]{:S(2)}, u32[]{:S(2)}) %collective-permute-start.22) | collective-permute-done | bytes 426016 | tf_op jit(solution)/shard_map/ppermute | solution.py:150
  195.4 7.9 %collective-permute-start.26 = (f32[64]{0:T(128)S(1)}, f32[64]{0:T(128)S(1)}, u32[]{:S(2)}, u32[]{:S(2)}) collective-permute-start(f32[64]{0:T(128)S(1)} %add.365), channel_id=1, source_target_pairs={{0,1},{1,2},{2,3},{3,0},{4,5},{5,6},{6,7},{7,4},{8,9},{9,10},{10,1... | collective-permute-start | bytes 776 | tf_op jit(solution)/shard_map/ppermute | solution.py:294
  205.5 2.9 collective-permute-start.28
  212.4 3.3 slice_bitcast_fusion
  217.8 37.4 %copy.22 = bf16[512,8,2,3328]{3,1,2,0:T(8,128)(2,1)} copy(bf16[512,8,2,3328]{3,2,1,0:T(2,128)(2,1)} %bitcast.185) | data formatting | bytes 109051904
  255.2 16.2 %shard_map.95.refs_0_ = f32[256,4096]{1,0:T(8,128)} custom-call(bf16[256,3328]{1,0:T(8,128)(2,1)} %all-gather.3.cloned.1.call-done.grads_ref, bf16[4096,6656]{1,0:T(8,128)(2,1)} %bitcast.181, bf16[4096,6656]{1,0:T(8,128)(2,1)} %bitcast.182), custom_call_target="tpu_custom_call" | custom-call | flops 6979321856 | bytes 33161216 | tf_op jit(solution)/shard_map/pallas_call | solution.py:191
  271.4 17.3 %shard_map.96 = f32[256,4096]{1,0:T(8,128)} custom-call(bf16[256,3328]{1,0:T(8,128)(2,1)} %all-gather.5.cloned.1.call-done.grads_ref, bf16[4096,6656]{1,0:T(8,128)(2,1)} %bitcast.183, bf16[4096,6656]{1,0:T(8,128)(2,1)} %bitcast.184, f32[256,4096]{1,0:T(8,128)} %shard_map.95.refs_0_), custom_call_target="tpu_custom_call", output_to_operand_aliasing={{}: (3, {})} | custom-call | flops 6979321856 | bytes 33161216 | tf_op jit(solution)/shard_map/pallas_call | solution.py:191
  290.6 2.6 collective-permute-done.32
  299.6 6.7 %collective-permute-done.35 = bf16[32,4096]{1,0:T(8,128)(2,1)} collective-permute-done((bf16[32,4096]{1,0:T(8,128)(2,1)}, bf16[32,4096]{1,0:T(8,128)(2,1)}, u32[]{:S(2)}, u32[]{:S(2)}) %collective-permute-start.35) | collective-permute-done | bytes 262176 | tf_op jit(solution)/shard_map/ppermute | solution.py:83
  306.4 4.7 %collective-permute-done.34 = bf16[32,4096]{1,0:T(8,128)(2,1)} collective-permute-done((bf16[32,4096]{1,0:T(8,128)(2,1)}, bf16[32,4096]{1,0:T(8,128)(2,1)}, u32[]{:S(2)}, u32[]{:S(2)}) %collective-permute-start.34) | collective-permute-done | bytes 262176 | tf_op jit(solution)/shard_map/ppermute | solution.py:83
  318.4 5.8 %collective-permute-done.36 = bf16[32,4096]{1,0:T(8,128)(2,1)S(1)} collective-permute-done((bf16[32,4096]{1,0:T(8,128)(2,1)}, bf16[32,4096]{1,0:T(8,128)(2,1)S(1)}, u32[]{:S(2)}, u32[]{:S(2)}) %collective-permute-start.36) | collective-permute-done | bytes 262176 | tf_op jit(solution)/shard_map/ppermute | solution.py:83
  324.2 4.7 %collective-permute-done.37 = bf16[32,4096]{1,0:T(8,128)(2,1)S(1)} collective-permute-done((bf16[32,4096]{1,0:T(8,128)(2,1)}, bf16[32,4096]{1,0:T(8,128)(2,1)S(1)}, u32[]{:S(2)}, u32[]{:S(2)}) %collective-permute-start.37) | collective-permute-done | bytes 262176 | tf_op jit(solution)/shard_map/ppermute | solution.py:83
  329.4 2.3 collective-permute-done.39
  331.8 17.4 %fusion.63 = f32[2560,4096]{1,0:T(8,128)} fusion(bf16[256,2560]{1,0:T(8,128)(2,1)S(1)} %bitcast.192, bf16[256,4096]{1,0:T(8,128)(2,1)S(1)} %bitcast.191), kind=kOutput, calls=%fused_computation.169 | convolution fusion | flops 5368709120 | bytes 45350912 | tf_op jit(solution)/shard_map/dot_general | solution.py:324
  349.2 31.8 %reduce-scatter.2.cloned.1.call-done = bf16[64,6656]{1,0:T(8,128)(2,1)} async-done(((bf16[256,6656]{1,0:T(8,128)(2,1)}), bf16[64,6656]{1,0:T(8,128)(2,1)}) %reduce-scatter.2.cloned.1.call-update) | async-done | bytes 851984 | tf_op jit(solution)/shard_map/reduce_scatter | solution.py:331
  (186 shorter events, 76.9 us)
Async XLA Ops:
  7.2 248.0 %all-gather.3.cloned.1.call-start = ((), (), s32[]{:S(2)}) async-start(), calls=%async_computation.1 | async-start | bytes 2129920 | tf_op jit(solution)/shard_map/all_gather | solution.py:279
  10.5 52.3 %collective-permute-start.4 = (bf16[1,64,4096]{2,1,0:T(8,128)(2,1)}, bf16[1,64,4096]{2,1,0:T(8,128)(2,1)}, u32[]{:S(2)}, u32[]{:S(2)}) collective-permute-start(bf16[1,64,4096]{2,1,0:T(8,128)(2,1)} %fusion.57), channel_id=1, source_target_pairs={{0,16},{8,24},{16,0},{24,8},{1,17},{9,25},{17,1},{25,9},{2,18},{10... | collective-permute-start | bytes 1572872 | tf_op jit(solution)/shard_map/ppermute | solution.py:28
  21.5 10.6 %collective-permute-start.1 = (f16[64,2048]{1,0:T(8,128)(2,1)}, f16[64,2048]{1,0:T(8,128)(2,1)}, u32[]{:S(2)}, u32[]{:S(2)}) collective-permute-start(f16[64,2048]{1,0:T(8,128)(2,1)} %get-tuple-element.92), channel_id=1, source_target_pairs={{0,4},{4,0},{1,5},{5,1},{2,6},{6,2},{3,7},{7,3},{8,12},{12,8},{9,1... | collective-permute-start | bytes 786440 | tf_op jit(solution)/shard_map/ppermute | solution.py:28
  29.9 7.8 %collective-permute-start = (f16[64,2048]{1,0:T(8,128)(2,1)}, f16[64,2048]{1,0:T(8,128)(2,1)}, u32[]{:S(2)}, u32[]{:S(2)}) collective-permute-start(f16[64,2048]{1,0:T(8,128)(2,1)} %get-tuple-element.94), channel_id=1, source_target_pairs={{0,4},{4,0},{1,5},{5,1},{2,6},{6,2},{3,7},{7,3},{8,12},{12,8},{9,1... | collective-permute-start | bytes 786440 | tf_op jit(solution)/shard_map/ppermute | solution.py:28
  39.3 5.5 %collective-permute-start.8 = (f32[128]{0:T(128)S(1)}, f32[128]{0:T(128)S(1)}, u32[]{:S(2)}, u32[]{:S(2)}) collective-permute-start(f32[128]{0:T(128)S(1)} %pad_maximum_fusion.6), channel_id=1, source_target_pairs={{0,3},{1,0},{2,1},{3,2},{4,7},{5,4},{6,5},{7,6},{8,11},{9,8},{10,9... | collective-permute-start | bytes 1544 | tf_op jit(solution)/shard_map/ppermute | solution.py:121
  42.9 5.4 %collective-permute-start.6 = (f32[128]{0:T(128)S(1)}, f32[128]{0:T(128)S(1)}, u32[]{:S(2)}, u32[]{:S(2)}) collective-permute-start(f32[128]{0:T(128)S(1)} %pad_maximum_fusion.6), channel_id=1, source_target_pairs={{0,1},{1,2},{2,3},{3,0},{4,5},{5,6},{6,7},{7,4},{8,9},{9,10},{10,1... | collective-permute-start | bytes 1544 | tf_op jit(solution)/shard_map/ppermute | solution.py:121
  49.2 16.4 %collective-permute-start.2 = (f16[1,64,4096]{2,1,0:T(8,128)(2,1)}, f16[1,64,4096]{2,1,0:T(8,128)(2,1)}, u32[]{:S(2)}, u32[]{:S(2)}) collective-permute-start(f16[1,64,4096]{2,1,0:T(8,128)(2,1)} %fusion.56), channel_id=1, source_target_pairs={{0,16},{8,24},{16,0},{24,8},{1,17},{9,25},{17,1},{25,9},{2,18},{10... | collective-permute-start | bytes 1572872 | tf_op jit(solution)/shard_map/ppermute | solution.py:28
  50.7 11.9 %collective-permute-start.11 = (f32[128]{0:T(128)S(1)}, f32[128]{0:T(128)S(1)}, u32[]{:S(2)}, u32[]{:S(2)}) collective-permute-start(f32[128]{0:T(128)S(1)} %add_rsqrt_fusion), channel_id=1, source_target_pairs={{0,24},{8,16},{16,8},{24,0},{1,25},{9,17},{17,9},{25,1},{2,26},{10... | collective-permute-start | bytes 1544 | tf_op jit(solution)/shard_map/ppermute | solution.py:28
  120.5 12.3 %collective-permute-start.15 = (f16[64,3328]{1,0:T(8,128)(2,1)S(1)}, f16[64,3328]{1,0:T(8,128)(2,1)S(1)}, u32[]{:S(2)}, u32[]{:S(2)}) collective-permute-start(f16[64,3328]{1,0:T(8,128)(2,1)S(1)} %fusion.25), channel_id=1, source_target_pairs={{3,2},{7,6},{11,10},{15,14},{19,18},{23,22},{27,26},{31,30}} | collective-permute-start | bytes 1277960 | tf_op jit(solution)/shard_map/ppermute | solution.py:151
  121.3 12.4 %collective-permute-start.12 = (f16[64,3328]{1,0:T(8,128)(2,1)S(1)}, f16[64,3328]{1,0:T(8,128)(2,1)S(1)}, u32[]{:S(2)}, u32[]{:S(2)}) collective-permute-start(f16[64,3328]{1,0:T(8,128)(2,1)S(1)} %fusion.15), channel_id=1, source_target_pairs={{0,1},{4,5},{8,9},{12,13},{16,17},{20,21},{24,25},{28,29}} | collective-permute-start | bytes 1277960 | tf_op jit(solution)/shard_map/ppermute | solution.py:150
  122.8 9.8 %collective-permute-start.18 = (bf16[1,64,2560]{2,1,0:T(8,128)(2,1)S(1)}, bf16[1,64,2560]{2,1,0:T(8,128)(2,1)S(1)}, u32[]{:S(2)}, u32[]{:S(2)}) collective-permute-start(bf16[1,64,2560]{2,1,0:T(8,128)(2,1)S(1)} %bitcast.196), channel_id=1, source_target_pairs={{0,16},{8,24},{16,0},{24,8},{1,17},{9,25},{17,1},{25,9},{2,18},{10... | collective-permute-start | bytes 983048 | tf_op jit(solution)/shard_map/ppermute | solution.py:28
  124.4 13.0 %collective-permute-start.23 = (f16[64,3328]{1,0:T(8,128)(2,1)S(1)}, f16[64,3328]{1,0:T(8,128)(2,1)S(1)}, u32[]{:S(2)}, u32[]{:S(2)}) collective-permute-start(f16[64,3328]{1,0:T(8,128)(2,1)S(1)} %fusion.36), channel_id=1, source_target_pairs={{3,2},{7,6},{11,10},{15,14},{19,18},{23,22},{27,26},{31,30}} | collective-permute-start | bytes 1277960 | tf_op jit(solution)/shard_map/ppermute | solution.py:151
  125.2 16.8 %collective-permute-start.20 = (f16[64,3328]{1,0:T(8,128)(2,1)S(1)}, f16[64,3328]{1,0:T(8,128)(2,1)S(1)}, u32[]{:S(2)}, u32[]{:S(2)}) collective-permute-start(f16[64,3328]{1,0:T(8,128)(2,1)S(1)} %fusion.26), channel_id=1, source_target_pairs={{0,1},{4,5},{8,9},{12,13},{16,17},{20,21},{24,25},{28,29}} | collective-permute-start | bytes 1277960 | tf_op jit(solution)/shard_map/ppermute | solution.py:150
  132.6 25.5 %collective-permute-start.19 = (bf16[2,64,2560]{2,1,0:T(8,128)(2,1)S(1)}, bf16[2,64,2560]{2,1,0:T(8,128)(2,1)S(1)}, u32[]{:S(2)}, u32[]{:S(2)}) collective-permute-start(bf16[2,64,2560]{2,1,0:T(8,128)(2,1)S(1)} %bitcast.195), channel_id=1, source_target_pairs={{0,8},{8,0},{16,24},{24,16},{1,9},{9,1},{17,25},{25,17},{2,10},{10... | collective-permute-start | bytes 1966088 | tf_op jit(solution)/shard_map/ppermute | solution.py:28
  133.0 14.3 %collective-permute-start.16 = (f16[64,3328]{1,0:T(8,128)(2,1)S(1)}, f16[64,3328]{1,0:T(8,128)(2,1)S(1)}, u32[]{:S(2)}, u32[]{:S(2)}) collective-permute-start(f16[64,3328]{1,0:T(8,128)(2,1)S(1)} %fusion.24), channel_id=1, source_target_pairs={{3,2},{2,1},{7,6},{6,5},{11,10},{10,9},{15,14},{14,13},{19,18},{18... | collective-permute-start | bytes 1277960 | tf_op jit(solution)/shard_map/ppermute | solution.py:151
  133.9 17.2 %collective-permute-start.13 = (f16[64,3328]{1,0:T(8,128)(2,1)S(1)}, f16[64,3328]{1,0:T(8,128)(2,1)S(1)}, u32[]{:S(2)}, u32[]{:S(2)}) collective-permute-start(f16[64,3328]{1,0:T(8,128)(2,1)S(1)} %fusion.17), channel_id=1, source_target_pairs={{0,1},{1,2},{4,5},{5,6},{8,9},{9,10},{12,13},{13,14},{16,17},{17,1... | collective-permute-start | bytes 1277960 | tf_op jit(solution)/shard_map/ppermute | solution.py:150
  137.6 18.1 %collective-permute-start.24 = (f16[64,3328]{1,0:T(8,128)(2,1)S(1)}, f16[64,3328]{1,0:T(8,128)(2,1)S(1)}, u32[]{:S(2)}, u32[]{:S(2)}) collective-permute-start(f16[64,3328]{1,0:T(8,128)(2,1)S(1)} %fusion.35), channel_id=1, source_target_pairs={{3,2},{2,1},{7,6},{6,5},{11,10},{10,9},{15,14},{14,13},{19,18},{18... | collective-permute-start | bytes 1277960 | tf_op jit(solution)/shard_map/ppermute | solution.py:151
  142.1 29.1 %collective-permute-start.21 = (f16[64,3328]{1,0:T(8,128)(2,1)S(1)}, f16[64,3328]{1,0:T(8,128)(2,1)}, u32[]{:S(2)}, u32[]{:S(2)}) collective-permute-start(f16[64,3328]{1,0:T(8,128)(2,1)S(1)} %fusion.28), channel_id=1, source_target_pairs={{0,1},{1,2},{4,5},{5,6},{8,9},{9,10},{12,13},{13,14},{16,17},{17,1... | collective-permute-start | bytes 1277960 | tf_op jit(solution)/shard_map/ppermute | solution.py:150
  147.5 12.9 %collective-permute-start.17 = (f16[64,3328]{1,0:T(8,128)(2,1)S(1)}, f16[64,3328]{1,0:T(8,128)(2,1)S(1)}, u32[]{:S(2)}, u32[]{:S(2)}) collective-permute-start(f16[64,3328]{1,0:T(8,128)(2,1)S(1)} %fusion.22), channel_id=1, source_target_pairs={{3,2},{2,1},{1,0},{7,6},{6,5},{5,4},{11,10},{10,9},{9,8},{15,14},{... | collective-permute-start | bytes 1277960 | tf_op jit(solution)/shard_map/ppermute | solution.py:151
  151.3 17.5 %collective-permute-start.14 = (f16[64,3328]{1,0:T(8,128)(2,1)S(1)}, f16[64,3328]{1,0:T(8,128)(2,1)S(1)}, u32[]{:S(2)}, u32[]{:S(2)}) collective-permute-start(f16[64,3328]{1,0:T(8,128)(2,1)S(1)} %fusion.19), channel_id=1, source_target_pairs={{0,1},{1,2},{2,3},{4,5},{5,6},{6,7},{8,9},{9,10},{10,11},{12,13},{... | collective-permute-start | bytes 1277960 | tf_op jit(solution)/shard_map/ppermute | solution.py:150
  156.6 20.3 %collective-permute-start.25 = (f16[64,3328]{1,0:T(8,128)(2,1)}, f16[64,3328]{1,0:T(8,128)(2,1)S(1)}, u32[]{:S(2)}, u32[]{:S(2)}) collective-permute-start(f16[64,3328]{1,0:T(8,128)(2,1)} %fusion.33), channel_id=1, source_target_pairs={{3,2},{2,1},{1,0},{7,6},{6,5},{5,4},{11,10},{10,9},{9,8},{15,14},{... | collective-permute-start | bytes 1277960 | tf_op jit(solution)/shard_map/ppermute | solution.py:151
  171.2 100.2 %all-gather.5.cloned.1.call-start = ((), (), s32[]{:S(2)}) async-start(), calls=%async_computation.2 | async-start | bytes 2129920 | tf_op jit(solution)/shard_map/all_gather | solution.py:279
  172.4 20.0 %collective-permute-start.22 = (f16[64,3328]{1,0:T(8,128)(2,1)S(1)}, f16[64,3328]{1,0:T(8,128)(2,1)S(1)}, u32[]{:S(2)}, u32[]{:S(2)}) collective-permute-start(f16[64,3328]{1,0:T(8,128)(2,1)S(1)} %fusion.30), channel_id=1, source_target_pairs={{0,1},{1,2},{2,3},{4,5},{5,6},{6,7},{8,9},{9,10},{10,11},{12,13},{... | collective-permute-start | bytes 1277960 | tf_op jit(solution)/shard_map/ppermute | solution.py:150
  195.4 13.1 %collective-permute-start.26 = (f32[64]{0:T(128)S(1)}, f32[64]{0:T(128)S(1)}, u32[]{:S(2)}, u32[]{:S(2)}) collective-permute-start(f32[64]{0:T(128)S(1)} %add.365), channel_id=1, source_target_pairs={{0,1},{1,2},{2,3},{3,0},{4,5},{5,6},{6,7},{7,4},{8,9},{9,10},{10,1... | collective-permute-start | bytes 776 | tf_op jit(solution)/shard_map/ppermute | solution.py:294
  209.8 171.2 %reduce-scatter.2.cloned.1.call-start = ((), (), s32[]{:S(2)}) async-start(), calls=%async_computation.3 | async-start | bytes 4259840 | tf_op jit(solution)/shard_map/reduce_scatter | solution.py:331
  215.7 39.4 %collective-permute-start.31 = (f32[4,64]{1,0:T(4,128)S(1)}, f32[4,64]{1,0:T(4,128)S(1)}, u32[]{:S(2)}, u32[]{:S(2)}) collective-permute-start(f32[4,64]{1,0:T(4,128)S(1)} %add.374), channel_id=1, source_target_pairs={{0,4},{4,0},{1,5},{5,1},{2,6},{6,2},{3,7},{7,3},{8,12},{12,8},{9,1... | collective-permute-start | bytes 3080 | tf_op jit(solution)/shard_map/ppermute | solution.py:28
  295.9 10.4 %collective-permute-start.35 = (bf16[32,4096]{1,0:T(8,128)(2,1)}, bf16[32,4096]{1,0:T(8,128)(2,1)}, u32[]{:S(2)}, u32[]{:S(2)}) collective-permute-start(bf16[32,4096]{1,0:T(8,128)(2,1)} %get-tuple-element.85), channel_id=1, source_target_pairs={{0,20},{4,16},{8,28},{12,24},{16,4},{20,0},{24,12},{28,8},{1,21},{... | collective-permute-start | bytes 786440 | tf_op jit(solution)/shard_map/ppermute | solution.py:83
  298.0 13.1 %collective-permute-start.34 = (bf16[32,4096]{1,0:T(8,128)(2,1)}, bf16[32,4096]{1,0:T(8,128)(2,1)}, u32[]{:S(2)}, u32[]{:S(2)}) collective-permute-start(bf16[32,4096]{1,0:T(8,128)(2,1)} %get-tuple-element.86), channel_id=1, source_target_pairs={{0,4},{4,0},{8,12},{12,8},{16,20},{20,16},{24,28},{28,24},{1,5},{5... | collective-permute-start | bytes 786440 | tf_op jit(solution)/shard_map/ppermute | solution.py:83
  298.1 13.6 %collective-permute-start.33 = (bf16[32,4096]{1,0:T(8,128)(2,1)}, bf16[32,4096]{1,0:T(8,128)(2,1)}, u32[]{:S(2)}, u32[]{:S(2)}) collective-permute-start(bf16[32,4096]{1,0:T(8,128)(2,1)} %get-tuple-element.84), channel_id=1, source_target_pairs={{0,16},{4,20},{8,24},{12,28},{16,0},{20,4},{24,8},{28,12},{1,17},{... | collective-permute-start | bytes 786440 | tf_op jit(solution)/shard_map/ppermute | solution.py:83
  314.8 9.4 %collective-permute-start.36 = (bf16[32,4096]{1,0:T(8,128)(2,1)}, bf16[32,4096]{1,0:T(8,128)(2,1)S(1)}, u32[]{:S(2)}, u32[]{:S(2)}) collective-permute-start(bf16[32,4096]{1,0:T(8,128)(2,1)} %get-tuple-element.45), channel_id=1, source_target_pairs={{0,16},{4,20},{8,24},{12,28},{16,0},{20,4},{24,8},{28,12},{1,17},{... | collective-permute-start | bytes 786440 | tf_op jit(solution)/shard_map/ppermute | solution.py:83
  315.5 13.4 %collective-permute-start.37 = (bf16[32,4096]{1,0:T(8,128)(2,1)}, bf16[32,4096]{1,0:T(8,128)(2,1)S(1)}, u32[]{:S(2)}, u32[]{:S(2)}) collective-permute-start(bf16[32,4096]{1,0:T(8,128)(2,1)} %get-tuple-element.45), channel_id=1, source_target_pairs={{0,4},{4,0},{8,12},{12,8},{16,20},{20,16},{24,28},{28,24},{1,5},{5... | collective-permute-start | bytes 786440 | tf_op jit(solution)/shard_map/ppermute | solution.py:83
  316.9 12.1 %collective-permute-start.38 = (bf16[32,4096]{1,0:T(8,128)(2,1)}, bf16[32,4096]{1,0:T(8,128)(2,1)S(1)}, u32[]{:S(2)}, u32[]{:S(2)}) collective-permute-start(bf16[32,4096]{1,0:T(8,128)(2,1)} %get-tuple-element.45), channel_id=1, source_target_pairs={{0,20},{4,16},{8,28},{12,24},{16,4},{20,0},{24,12},{28,8},{1,21},{... | collective-permute-start | bytes 786440 | tf_op jit(solution)/shard_map/ppermute | solution.py:83
  (24 other events, 213.1 us)
Sparse Core Ops, SparseCore 0:
  171.3 42.1 all-gather.2
  215.7 39.7 all-gather.4
  315.6 65.3 reduce-scatter.1
